TPU v7x, 512 devices: a whole 4x4x16 slice. The times are simulated.
512 devices in a mesh: vel: 64 (over x_lo, z, core), box: 8 (over x_hi, y).
Axes of the slice: x: 4 (x_hi: 2, x_lo: 2; x = x_hi * 2 + x_lo), y: 4, z: 16, core: 2. Of those that a mesh axis runs over, the one named last changes fastest.
Arguments:
- distribution: float32 [4096, 3, 3, 3, 8, 128], P('vel', None, None, None, 'box'), may hold values from -2.5 to 2.5, as said below
- collision_rate: float32 [8, 128], P('box'), may hold values from 1 to 10
Outputs:
- advanced: float32 [4096, 3, 3, 3, 8, 128], P('vel', None, None, None, 'box')
Inputs may be any that keep to these rules, and one draw needn't show every extreme that they name: `distribution`: coefficient (0,0,0) is positive for every box and velocity; every other coefficient is at most coefficient (0,0,0) of the same box and velocity in magnitude.
All inputs are finite; a program needn't handle non-finite values.
Results may differ from a plain program's by a relative error of at most 0.0003.
Values sent between devices are 32-bit elements; how exact they have to be, the bound alone decides.
No kernel may reach another device: no remote copies, remote signals or barrier semaphores. Data moves between devices by JAX's collectives and lax.ppermute only.
A program may use at most 64 MiB of HBM per device.

v0:
```python
import math

import jax
import jax.numpy as jnp
from jax import lax
from jax.experimental import pallas as pl
from jax.experimental.pallas import tpu as pltpu
from jax.sharding import PartitionSpec as P


NZ = 16
VELS = 64
BOXES = 8
COUNT = 64
STEP = 0.02
SPACING = 0.5
FIRST = -3.75
WEIGHT = SPACING**3
ROWS = 16
TILE = 8
GRANT = 16 << 20
CHUNK = COUNT * 27 // 4


def mode(a, b, c):
    return 9 * a + 3 * b + c


def row_index():
    return lax.broadcasted_iota(jnp.int32, (TILE, 128), 0)


class Place:
    def __init__(self):
        self.vel = lax.axis_index("vel")
        self.box = lax.axis_index("box")
        right = self.vel >= VELS // 2
        self.sx = jnp.where(right, 1.0, -1.0)
        self.wx = (self.vel // 4).astype(jnp.float32) * SPACING + FIRST
        self.ax = self.wx * self.sx
        up = self.vel % 4 >= 2
        self.sy = jnp.where(up, 1.0, -1.0)
        self.first_y = (self.vel % 4 * 4).astype(jnp.float32) * SPACING + FIRST
        self.shift_y = jnp.where(up, NZ, 128 - NZ)
        self.upwind = jnp.where(right, (self.box + BOXES - 1) % BOXES, (self.box + 1) % BOXES)
        self.downwind = jnp.where(right, (self.box + 1) % BOXES, (self.box + BOXES - 1) % BOXES)
        self.lane = lax.broadcasted_iota(jnp.int32, (TILE, 128), 1) % NZ

    def wy(self, j):
        return self.first_y + j.astype(jnp.float32) * SPACING

    def wz(self, half):
        return row_index().astype(jnp.float32) * SPACING + (FIRST + half * TILE * SPACING)

    def from_y(self, values):
        return pltpu.roll(values, self.shift_y, 1)

    def from_z(self, values, half):
        if half:
            return jnp.where(self.lane == 0, pltpu.roll(values, 128 + 1 - NZ, 1), pltpu.roll(values, 1, 1))
        return jnp.where(self.lane == NZ - 1, pltpu.roll(values, NZ - 1, 1), pltpu.roll(values, 127, 1))


def trace(low, middle, high, sign):
    return low + sign * middle + high


def trace_z(low, middle, high, half):
    return low + middle + high if half else low - middle + high


def one_direction(rates, coefs, index, upper, inflow, speed, size):
    _, i1, i2 = index
    jump = inflow - upper
    parts = (
        size * jump,
        (-3.0 * speed) * jump - (6.0 * size) * coefs[i1] - (6.0 * speed) * coefs[i2],
        (5.0 * size) * jump + (10.0 * speed) * coefs[i1],
    )
    for i, part in zip(index, parts):
        rates[i] = part if rates[i] is None else rates[i] + part


def transport(place, coefs, inflow_x, j, half):
    rates = [None] * 27
    for b in range(3):
        for c in range(3):
            index = [mode(a, b, c) for a in range(3)]
            upper = trace(*(coefs[i] for i in index), place.sx)
            one_direction(rates, coefs, index, upper, inflow_x[3 * b + c], place.wx, place.ax)
    wy = place.wy(j)
    ay = wy * place.sy
    for a in range(3):
        for c in range(3):
            index = [mode(a, b, c) for b in range(3)]
            upper = trace(*(coefs[i] for i in index), place.sy)
            one_direction(rates, coefs, index, upper, place.from_y(upper), wy, ay)
    wz = place.wz(half)
    az = wz if half else -wz
    for a in range(3):
        for b in range(3):
            index = [mode(a, b, c) for c in range(3)]
            upper = trace_z(*(coefs[i] for i in index), half)
            one_direction(rates, coefs, index, upper, place.from_z(upper, half), wz, az)
    return rates


def velocity_groups(body):
    def step(j, carry):
        for half in range(2):
            carry = body(j, half, pl.multiple_of((2 * j + half) * TILE, TILE), carry)
        return carry

    return step


def load_coefs(field, start):
    return [field[pl.ds(start * 27 + m, TILE, stride=27), :] for m in range(27)]


def moments(place, j, half, values):
    wy = place.wy(j)
    wz = place.wz(half)
    energy = 0.5 * (place.wx * place.wx + wy * wy + wz * wz)
    return [values, place.wx * values, wy * values, wz * values, energy * values]


def stack_rows(rows):
    index = row_index()
    tile = jnp.zeros((TILE, 128), jnp.float32)
    for i, row in enumerate(rows):
        tile = jnp.where(index == i, jnp.broadcast_to(row, (TILE, 128)), tile)
    return tile


def chunk_copy(source, target, sems, j):
    rows = pl.ds(pl.multiple_of(j * CHUNK, CHUNK), CHUNK)
    return pltpu.make_async_copy(source.at[rows], target.at[rows], sems.at[j])


def first_kernel(field_hbm, rate_hbm, halo, column, field, rate, sems):
    place = Place()
    for j in range(4):
        chunk_copy(field_hbm, field, sems, j).start()
    rate_copy = pltpu.make_async_copy(rate_hbm, rate, sems.at[4])
    rate_copy.start()

    def body(j, half, start, sums):
        if not half:
            chunk_copy(field_hbm, field, sems, j).wait()
        coefs = load_coefs(field, start)
        for k in range(9):
            halo[pl.ds(k * COUNT + start, TILE), :] = trace(coefs[k], coefs[9 + k], coefs[18 + k], place.sx)
        base = coefs[0]
        out_x = place.ax * trace(base, coefs[9], coefs[18], place.sx)
        upper_y = trace(base, coefs[3], coefs[6], place.sy)
        upper_z = trace_z(base, coefs[1], coefs[2], half)
        wy = place.wy(j)
        wz = place.wz(half)
        kept = (wy * place.sy) * (place.from_y(upper_y) - upper_y) - out_x
        kept = kept + (wz if half else -wz) * (place.from_z(upper_z, half) - upper_z)
        terms = moments(place, j, half, base) + moments(place, j, half, kept) + moments(place, j, half, out_x)
        return tuple(s + t for s, t in zip(sums, terms))

    zero = jnp.zeros((TILE, 128), jnp.float32)
    sums = lax.fori_loop(0, 4, velocity_groups(body), (zero,) * 15)
    sums = [WEIGHT * jnp.sum(s, axis=0, keepdims=True) for s in sums]
    first = stack_rows(sums[:5] + sums[10:13])
    second = stack_rows(sums[5:10] + sums[13:])
    for p in range(NZ):
        column[p * ROWS : p * ROWS + TILE, :] = first
        column[p * ROWS + TILE : (p + 1) * ROWS, :] = second
    rate_copy.wait()


def between_kernel(column, rate, planes):
    place = Place()
    first = sum(column[p * ROWS : p * ROWS + TILE, :] for p in range(NZ))
    second = sum(column[p * ROWS + TILE : (p + 1) * ROWS, :] for p in range(NZ))
    index = row_index()
    held = jnp.where(index < 5, first, jnp.broadcast_to(rate[...], (TILE, 128)))
    gone = jnp.where(index < 3, pltpu.roll(first, 3, 0), pltpu.roll(second, TILE - 2, 0))
    for box in range(BOXES):
        sent = jnp.where(place.box == box, second, jnp.where(place.downwind == box, gone, 0.0))
        for q in range(4):
            start = (q * BOXES + box) * ROWS
            planes[start : start + TILE, :] = held
            planes[start + TILE : start + ROWS, :] = sent


def second_kernel(field, rate, halo, middle, halo_out):
    place = Place()
    collision = jnp.broadcast_to(rate[...], (TILE, 128))

    def body(j, half, start, carry):
        coefs = load_coefs(field, start)
        inflow = [halo[pl.ds(k * COUNT + start, TILE), :] for k in range(9)]
        rates = transport(place, coefs, inflow, j, half)
        new = [c + STEP * (r - collision * c) for c, r in zip(coefs, rates)]
        for m in range(27):
            middle[pl.ds(m * COUNT + start, TILE), :] = new[m]
        for k in range(9):
            halo_out[pl.ds(k * COUNT + start, TILE), :] = trace(new[k], new[9 + k], new[18 + k], place.sx)
        return carry

    lax.fori_loop(0, 4, velocity_groups(body), 0)


def states(totals):
    density = totals[0]
    flow = [t / density for t in totals[1:4]]
    square = flow[0] * flow[0] + flow[1] * flow[1] + flow[2] * flow[2]
    temper = (2.0 * totals[4] / density - square) / 3.0
    spread = 2.0 * math.pi * temper
    return flow, density / (spread * jnp.sqrt(spread)), 0.5 / temper


def maxwell_moments(state):
    flow, scale, inverse = state
    centres = lax.broadcasted_iota(jnp.int32, (16, 128), 0).astype(jnp.float32) * SPACING + FIRST
    sums = []
    for u in flow:
        offset = centres - u
        bell = jnp.exp(-(offset * offset) * inverse)
        sums.append([jnp.sum(v, axis=0, keepdims=True) for v in (bell, centres * bell, centres * centres * bell)])
    (x0, x1, x2), (y0, y1, y2), (z0, z1, z2) = sums
    scale = WEIGHT * scale
    energy = x2 * y0 * z0 + x0 * y2 * z0 + x0 * y0 * z2
    return [
        scale * (x0 * y0 * z0),
        scale * (x1 * y0 * z0),
        scale * (x0 * y1 * z0),
        scale * (x0 * y0 * z1),
        scale * (0.5 * energy),
    ]


def third_kernel(field, rate, halo, planes, middle, out_hbm, out, sems):
    place = Place()

    def of_box(box):
        return sum(planes[pl.ds(pl.multiple_of((q * BOXES + box) * ROWS, ROWS), TILE), :] for q in range(4))

    own = of_box(place.box)
    behind = of_box(place.upwind)
    kept = sum(planes[p * ROWS + TILE : (p + 1) * ROWS, :] for p in range(4 * BOXES))
    nu = rate[...]
    upwind_nu = planes[pl.ds(place.upwind * ROWS + 5, 1), :]
    totals, upwind, flux = ([tile[i : i + 1, :] for i in range(5)] for tile in (own, behind, kept))
    now = states(totals)
    gains = maxwell_moments(now)
    later = states([t + STEP * (f - nu * t + nu * g) for t, f, g in zip(totals, flux, gains)])
    before = states(upwind)

    def spread_out(state, factor):
        flow, scale, inverse = state
        wide = lambda v: jnp.broadcast_to(v, (TILE, 128))
        part = (place.wx - flow[0]) * (place.wx - flow[0])
        return wide(part), wide(flow[1]), wide(flow[2]), wide(factor * scale), wide(-inverse)

    now = spread_out(now, STEP * nu)
    before = spread_out(before, STEP * upwind_nu)
    later = spread_out(later, nu)
    collision = jnp.broadcast_to(nu, (TILE, 128))

    def body(j, half, start, carry):
        wy = place.wy(j)
        wz = place.wz(half)

        def bell(state):
            part, flow_y, flow_z, scale, inverse = state
            off_y = wy - flow_y
            off_z = wz - flow_z
            return scale * jnp.exp((part + off_y * off_y + off_z * off_z) * inverse)

        coefs = [middle[pl.ds(m * COUNT + start, TILE), :] for m in range(27)]
        coefs[0] = coefs[0] + bell(now)
        inflow = [halo[pl.ds(k * COUNT + start, TILE), :] for k in range(9)]
        inflow[0] = inflow[0] + bell(before)
        rates = transport(place, coefs, inflow, j, half)
        rates[0] = rates[0] + bell(later)
        for m in range(27):
            here = pl.ds(start * 27 + m, TILE, stride=27)
            moved = coefs[m] + STEP * (rates[m] - collision * coefs[m])
            out[here, :] = 0.5 * field[here, :] + 0.5 * moved
        if half:
            chunk_copy(out, out_hbm, sems, j).start()
        return carry

    lax.fori_loop(0, 4, velocity_groups(body), 0)
    for j in range(4):
        chunk_copy(out, out_hbm, sems, j).wait()


def call(kernel, outs, *args, remote_in=0, remote_out=False, scratch=()):
    vmem = pl.BlockSpec(memory_space=pltpu.VMEM)
    hbm = pl.BlockSpec(memory_space=pltpu.HBM)
    shapes = [jax.ShapeDtypeStruct(s, jnp.float32) for s in outs]
    moved = sum(4 * math.prod(s) for s in outs) + sum(4 * a.size for a in args)
    return pl.pallas_call(
        kernel,
        out_shape=shapes,
        in_specs=[hbm] * remote_in + [vmem] * (len(args) - remote_in),
        out_specs=[hbm if remote_out else vmem] * len(outs),
        scratch_shapes=scratch,
        compiler_params=pltpu.CompilerParams(vmem_limit_bytes=GRANT),
        cost_estimate=pl.CostEstimate(flops=4000000, bytes_accessed=moved, transcendentals=30000),
    )(*args)


def downwind_pairs():
    pairs = []
    for vel in range(VELS):
        step = 1 if vel >= VELS // 2 else BOXES - 1
        for box in range(BOXES):
            pairs.append((vel * BOXES + box, vel * BOXES + (box + step) % BOXES))
    return pairs


def vel_of(x, z, core):
    return x * 32 + z * 2 + core


PLANES = [
    [vel_of(x, z, core) * BOXES + box for x in range(2) for core in range(2) for box in range(BOXES)]
    for z in range(NZ)
]
COLUMNS = [[vel_of(x, (z + 8) % NZ, core) for z in range(NZ)] for x in range(2) for core in range(2)]


def exchange(blocks, axis, groups):
    count = len(groups[0])
    blocks = blocks.reshape(count, ROWS, 128)
    blocks = lax.all_to_all(blocks, axis, 0, 0, axis_index_groups=groups)
    return blocks.reshape(count * ROWS, 128)


def step(distribution, collision_rate):
    field = pltpu.with_memory_space_constraint(distribution.reshape(COUNT * 27, 128), pltpu.HBM)
    collision_rate = pltpu.with_memory_space_constraint(collision_rate, pltpu.HBM)
    face = (9 * COUNT, 128)
    whole = (27 * COUNT, 128)
    halo, column, field, rate = call(
        first_kernel,
        [face, (NZ * ROWS, 128), whole, (1, 128)],
        field,
        collision_rate,
        remote_in=2,
        scratch=[pltpu.SemaphoreType.DMA((5,))],
    )
    halo = lax.ppermute(halo, ("vel", "box"), downwind_pairs())
    column = exchange(column, "vel", COLUMNS)
    middle, halo = call(second_kernel, [whole, face], field, rate, halo)
    halo = lax.ppermute(halo, ("vel", "box"), downwind_pairs())
    (planes,) = call(between_kernel, [(4 * BOXES * ROWS, 128)], column, rate)
    planes = exchange(planes, ("vel", "box"), PLANES)
    (out,) = call(
        third_kernel,
        [whole],
        field,
        rate,
        halo,
        planes,
        middle,
        remote_out=True,
        scratch=[pltpu.VMEM(whole, jnp.float32), pltpu.SemaphoreType.DMA((4,))],
    )
    return out.reshape(distribution.shape)


def solution(mesh):
    return jax.shard_map(
        step,
        mesh=mesh,
        in_specs=(P("vel", None, None, None, "box", None), P("box", None)),
        out_specs=P("vel", None, None, None, "box", None),
        check_vma=False,
    )
```

profile of v0, /device:TPU:1, one launch (start us, length us, event | category | flops | bytes accessed | tf_op | source)
XLA Modules:
  0.0 58.7 jit_solution(15048337681180799277)
XLA Ops:
  0.0 2.1 %shard_map.28 = (f32[576,128]{1,0:T(8,128)S(1)}, f32[256,128]{1,0:T(8,128)}, f32[1728,128]{1,0:T(8,128)S(1)}, f32[1,128]{1,0:T(1,128)S(1)}) custom-call(f32[1728,128]{1,0:T(8,128)} %bitcast.8, f32[1,128]{1,0:T(1,128)} %rate_hbm.1), custom_call_target="tpu_custom_call" | custom-call | flops 4000000 | bytes 2196480 | tf_op jit(solution)/shard_map/pallas_call | solution.py:300
  2.1 19.1 %all-to-all-start = ((f32[16,16,128]{2,1,0:T(8,128)}), f32[16,16,128]{2,1,0:T(8,128)S(1)}, u32[]{:S(2)}, u32[]{:S(2)}) async-start(f32[16,16,128]{2,1,0:T(8,128)} %bitcast.1), calls=%async_computation | async-start | bytes 262144 | tf_op jit(solution)/shard_map/all_to_all | solution.py:334
  21.2 7.1 %collective-permute-start = (f32[576,128]{1,0:T(8,128)S(1)}, f32[576,128]{1,0:T(8,128)S(1)}, u32[]{:S(2)}, u32[]{:S(2)}) collective-permute-start(f32[576,128]{1,0:T(8,128)S(1)} %get-tuple-element.13), channel_id=1, source_target_pairs={{0,7},{1,0},{2,1},{3,2},{4,3},{5,4},{6,5},{7,6},{8,15},{9,8},{10,9... | collective-permute-start | bytes 884744 | tf_op jit(solution)/shard_map/ppermute | solution.py:351
  28.3 5.1 %collective-permute-done.halo = f32[576,128]{1,0:T(8,128)S(1)} collective-permute-done((f32[576,128]{1,0:T(8,128)S(1)}, f32[576,128]{1,0:T(8,128)S(1)}, u32[]{:S(2)}, u32[]{:S(2)}) %collective-permute-start) | collective-permute-done | bytes 294944 | tf_op jit(solution)/shard_map/ppermute | solution.py:351
  33.4 0.7 %shard_map.29 = (f32[1728,128]{1,0:T(8,128)S(1)}, f32[576,128]{1,0:T(8,128)S(1)}) custom-call(f32[1728,128]{1,0:T(8,128)S(1)} %get-tuple-element.11.field, f32[1,128]{1,0:T(1,128)S(1)} %get-tuple-element.12.rate, f32[576,128]{1,0:T(8,128)S(1)} %collective-permute-done.halo), custom_call_target="tpu_custom_call" | custom-call | flops 4000000 | bytes 2359808 | tf_op jit(solution)/shard_map/pallas_call | solution.py:300
  34.1 7.7 %collective-permute-start.1 = (f32[576,128]{1,0:T(8,128)S(1)}, f32[576,128]{1,0:T(8,128)S(1)}, u32[]{:S(2)}, u32[]{:S(2)}) collective-permute-start(f32[576,128]{1,0:T(8,128)S(1)} %get-tuple-element.14), channel_id=1, source_target_pairs={{0,7},{1,0},{2,1},{3,2},{4,3},{5,4},{6,5},{7,6},{8,15},{9,8},{10,9... | collective-permute-start | bytes 884744 | tf_op jit(solution)/shard_map/ppermute | solution.py:354
  41.9 0.0 all-to-all-done
  41.9 0.7 %shard_map.30 = f32[512,128]{1,0:T(8,128)} custom-call(f32[256,128]{1,0:T(8,128)S(1)} %bitcast.7, f32[1,128]{1,0:T(1,128)S(1)} %get-tuple-element.12.rate), custom_call_target="tpu_custom_call" | custom-call | flops 4000000 | bytes 393728 | tf_op jit(solution)/shard_map/pallas_call | solution.py:300
  42.6 5.9 %all-to-all-start.1 = ((f32[32,16,128]{2,1,0:T(8,128)}), f32[32,16,128]{2,1,0:T(8,128)S(1)}, u32[]{:S(2)}, u32[]{:S(2)}) async-start(f32[32,16,128]{2,1,0:T(8,128)} %bitcast.3), calls=%async_computation.1 | async-start | bytes 524288 | tf_op jit(solution)/shard_map/all_to_all | solution.py:334
  48.6 0.0 collective-permute-done.1.halo
  48.6 8.5 %all-to-all-done.1 = f32[32,16,128]{2,1,0:T(8,128)S(1)} async-done(((f32[32,16,128]{2,1,0:T(8,128)}), f32[32,16,128]{2,1,0:T(8,128)S(1)}, u32[]{:S(2)}, u32[]{:S(2)}) %all-to-all-start.1) | async-done | bytes 262176 | tf_op jit(solution)/shard_map/all_to_all | solution.py:334
  57.0 1.7 %shard_map.31 = f32[1728,128]{1,0:T(8,128)} custom-call(f32[1728,128]{1,0:T(8,128)S(1)} %get-tuple-element.11.field, f32[1,128]{1,0:T(1,128)S(1)} %get-tuple-element.12.rate, f32[576,128]{1,0:T(8,128)S(1)} %collective-permute-done.1.halo, f32[512,128]{1,0:T(8,128)S(1)} %bitcast.6, f32[1728,128]{1,0:T(8,128)S(1)} %get-tuple-element.16.middle), custom_call_target="tpu_custom_call" | custom-call | flops 4000000 | bytes 3211776 | tf_op jit(solution)/shard_map/pallas_call | solution.py:300
Async XLA Ops:
  2.1 39.8 %all-to-all-start = ((f32[16,16,128]{2,1,0:T(8,128)}), f32[16,16,128]{2,1,0:T(8,128)S(1)}, u32[]{:S(2)}, u32[]{:S(2)}) async-start(f32[16,16,128]{2,1,0:T(8,128)} %bitcast.1), calls=%async_computation | async-start | bytes 262144 | tf_op jit(solution)/shard_map/all_to_all | solution.py:334
  21.2 12.2 %collective-permute-start = (f32[576,128]{1,0:T(8,128)S(1)}, f32[576,128]{1,0:T(8,128)S(1)}, u32[]{:S(2)}, u32[]{:S(2)}) collective-permute-start(f32[576,128]{1,0:T(8,128)S(1)} %get-tuple-element.13), channel_id=1, source_target_pairs={{0,7},{1,0},{2,1},{3,2},{4,3},{5,4},{6,5},{7,6},{8,15},{9,8},{10,9... | collective-permute-start | bytes 884744 | tf_op jit(solution)/shard_map/ppermute | solution.py:351
  34.1 14.4 %collective-permute-start.1 = (f32[576,128]{1,0:T(8,128)S(1)}, f32[576,128]{1,0:T(8,128)S(1)}, u32[]{:S(2)}, u32[]{:S(2)}) collective-permute-start(f32[576,128]{1,0:T(8,128)S(1)} %get-tuple-element.14), channel_id=1, source_target_pairs={{0,7},{1,0},{2,1},{3,2},{4,3},{5,4},{6,5},{7,6},{8,15},{9,8},{10,9... | collective-permute-start | bytes 884744 | tf_op jit(solution)/shard_map/ppermute | solution.py:354
  42.6 14.4 %all-to-all-start.1 = ((f32[32,16,128]{2,1,0:T(8,128)}), f32[32,16,128]{2,1,0:T(8,128)S(1)}, u32[]{:S(2)}, u32[]{:S(2)}) async-start(f32[32,16,128]{2,1,0:T(8,128)} %bitcast.3), calls=%async_computation.1 | async-start | bytes 524288 | tf_op jit(solution)/shard_map/all_to_all | solution.py:334
where the time goes:
time: 59.1 us; the launch traced here: 58.7 us
  starting transfers between devices  39.9 us (68%)
  waiting for transfers between devices  13.6 us (23%)
  Pallas kernels  5.23 us (9%)
    all_to_all x2, starting transfers between devices, exchange(): blocks = lax.all_to_all(blocks, axis, 0, 0, axis_index_groups=groups)  25.1 us
    ppermute x2, starting transfers between devices, step(): halo = lax.ppermute(halo, ('vel', 'box'), downwind_pairs())  14.8 us
    all_to_all x2, waiting for transfers between devices, exchange(): blocks = lax.all_to_all(blocks, axis, 0, 0, axis_index_groups=groups)  8.47 us
    pallas_call x4, Pallas kernels, call(): pl.pallas_call(kernel, out_shape=shapes, in_specs=[hbm] * remote_in + [vm...  5.23 us
    ppermute x2, waiting for transfers between devices, step(): halo = lax.ppermute(halo, ('vel', 'box'), downwind_pairs())  5.11 us
  transfers between devices with their start and end apart: 4, of which 2 were waited for; matrix products, arithmetic and copies ran while one was open for 0% of the time, Pallas kernels for 2%

commit v1 on v0

--- a/solution.py
+++ b/solution.py
@@ -9,17 +9,21 @@
 
 
 NZ = 16
+VPD = 16
 VELS = 64
+LEAD = 8
 BOXES = 8
 COUNT = 64
 STEP = 0.02
 SPACING = 0.5
 FIRST = -3.75
 WEIGHT = SPACING**3
-ROWS = 16
+COLUMN_ROWS = 12
+PLANE_ROWS = 10
 TILE = 8
 GRANT = 16 << 20
 CHUNK = COUNT * 27 // 4
+FACE = 9 * COUNT + TILE
 
 
 def mode(a, b, c):
@@ -121,20 +125,23 @@
 def moments(place, j, half, values):
     wy = place.wy(j)
     wz = place.wz(half)
-    energy = 0.5 * (place.wx * place.wx + wy * wy + wz * wz)
-    return [values, place.wx * values, wy * values, wz * values, energy * values]
-
-
-def stack_rows(rows):
-    index = row_index()
-    tile = jnp.zeros((TILE, 128), jnp.float32)
-    for i, row in enumerate(rows):
-        tile = jnp.where(index == i, jnp.broadcast_to(row, (TILE, 128)), tile)
-    return tile
-
-
-def chunk_copy(source, target, sems, j):
-    rows = pl.ds(pl.multiple_of(j * CHUNK, CHUNK), CHUNK)
+    return [values, wy * values, wz * values, (0.5 * (wy * wy + wz * wz)) * values]
+
+
+def all_moments(wx, four):
+    total = lambda values: jnp.sum(values, axis=0, keepdims=True)
+    count, along_y, along_z, energy = four
+    return [
+        total(count),
+        total(wx * count),
+        total(along_y),
+        total(along_z),
+        total(energy + (0.5 * (wx * wx)) * count),
+    ]
+
+
+def chunk_copy(source, target, sems, j, size=CHUNK):
+    rows = pl.ds(pl.multiple_of(j * size, size), size)
     return pltpu.make_async_copy(source.at[rows], target.at[rows], sems.at[j])
 
 
@@ -163,29 +170,25 @@
         return tuple(s + t for s, t in zip(sums, terms))
 
     zero = jnp.zeros((TILE, 128), jnp.float32)
-    sums = lax.fori_loop(0, 4, velocity_groups(body), (zero,) * 15)
+    sums = lax.fori_loop(0, 4, velocity_groups(body), (zero,) * 12)
     sums = [WEIGHT * jnp.sum(s, axis=0, keepdims=True) for s in sums]
-    first = stack_rows(sums[:5] + sums[10:13])
-    second = stack_rows(sums[5:10] + sums[13:])
-    for p in range(NZ):
-        column[p * ROWS : p * ROWS + TILE, :] = first
-        column[p * ROWS + TILE : (p + 1) * ROWS, :] = second
+    for i, row in enumerate(sums):
+        column[pl.ds(i, NZ, stride=COLUMN_ROWS), :] = jnp.broadcast_to(row, (NZ, 128))
     rate_copy.wait()
 
 
-def between_kernel(column, rate, planes):
+def between_kernel(column, planes):
     place = Place()
-    first = sum(column[p * ROWS : p * ROWS + TILE, :] for p in range(NZ))
-    second = sum(column[p * ROWS + TILE : (p + 1) * ROWS, :] for p in range(NZ))
-    index = row_index()
-    held = jnp.where(index < 5, first, jnp.broadcast_to(rate[...], (TILE, 128)))
-    gone = jnp.where(index < 3, pltpu.roll(first, 3, 0), pltpu.roll(second, TILE - 2, 0))
-    for box in range(BOXES):
-        sent = jnp.where(place.box == box, second, jnp.where(place.downwind == box, gone, 0.0))
-        for q in range(4):
-            start = (q * BOXES + box) * ROWS
-            planes[start : start + TILE, :] = held
-            planes[start + TILE : start + ROWS, :] = sent
+    source = lax.broadcasted_iota(jnp.int32, (NZ, 128), 0)
+    source = (source + LEAD) % NZ // 2 + place.vel // (VELS // 2) * (VPD // 2)
+    wx = source.astype(jnp.float32) * SPACING + FIRST
+    rows = [column[pl.ds(i, NZ, stride=COLUMN_ROWS), :] for i in range(COLUMN_ROWS)]
+    held, kept, gone = (all_moments(wx, rows[k : k + 4]) for k in (0, 4, 8))
+    for i in range(5):
+        planes[pl.ds(i, 4 * BOXES, stride=PLANE_ROWS), :] = jnp.broadcast_to(held[i], (4 * BOXES, 128))
+        box = lax.broadcasted_iota(jnp.int32, (4 * BOXES, 128), 0) % BOXES
+        sent = jnp.where(box == place.box, kept[i], jnp.where(box == place.downwind, gone[i], 0.0))
+        planes[pl.ds(5 + i, 4 * BOXES, stride=PLANE_ROWS), :] = sent
 
 
 def second_kernel(field, rate, halo, middle, halo_out):
@@ -204,6 +207,7 @@
         return carry
 
     lax.fori_loop(0, 4, velocity_groups(body), 0)
+    halo_out[FACE - TILE :, :] = collision
 
 
 def states(totals):
@@ -238,15 +242,14 @@
 def third_kernel(field, rate, halo, planes, middle, out_hbm, out, sems):
     place = Place()
 
-    def of_box(box):
-        return sum(planes[pl.ds(pl.multiple_of((q * BOXES + box) * ROWS, ROWS), TILE), :] for q in range(4))
-
-    own = of_box(place.box)
-    behind = of_box(place.upwind)
-    kept = sum(planes[p * ROWS + TILE : (p + 1) * ROWS, :] for p in range(4 * BOXES))
+    box = lax.broadcasted_iota(jnp.int32, (4 * BOXES, 128), 0) % BOXES
+    rows = [planes[pl.ds(i, 4 * BOXES, stride=PLANE_ROWS), :] for i in range(PLANE_ROWS)]
+    total = lambda values: jnp.sum(values, axis=0, keepdims=True)
+    totals = [total(jnp.where(box == place.box, r, 0.0)) for r in rows[:5]]
+    upwind = [total(jnp.where(box == place.upwind, r, 0.0)) for r in rows[:5]]
+    flux = [total(r) for r in rows[5:]]
     nu = rate[...]
-    upwind_nu = planes[pl.ds(place.upwind * ROWS + 5, 1), :]
-    totals, upwind, flux = ([tile[i : i + 1, :] for i in range(5)] for tile in (own, behind, kept))
+    upwind_nu = halo[FACE - 1 :, :]
     now = states(totals)
     gains = maxwell_moments(now)
     later = states([t + STEP * (f - nu * t + nu * g) for t, f, g in zip(totals, flux, gains)])
@@ -283,13 +286,12 @@
             here = pl.ds(start * 27 + m, TILE, stride=27)
             moved = coefs[m] + STEP * (rates[m] - collision * coefs[m])
             out[here, :] = 0.5 * field[here, :] + 0.5 * moved
-        if half:
-            chunk_copy(out, out_hbm, sems, j).start()
+        chunk_copy(out, out_hbm, sems, 2 * j + half, CHUNK // 2).start()
         return carry
 
     lax.fori_loop(0, 4, velocity_groups(body), 0)
-    for j in range(4):
-        chunk_copy(out, out_hbm, sems, j).wait()
+    for j in range(8):
+        chunk_copy(out, out_hbm, sems, j, CHUNK // 2).wait()
 
 
 def call(kernel, outs, *args, remote_in=0, remote_out=False, scratch=()):
@@ -325,24 +327,24 @@
     [vel_of(x, z, core) * BOXES + box for x in range(2) for core in range(2) for box in range(BOXES)]
     for z in range(NZ)
 ]
-COLUMNS = [[vel_of(x, (z + 8) % NZ, core) for z in range(NZ)] for x in range(2) for core in range(2)]
+COLUMNS = [[vel_of(x, (z + LEAD) % NZ, core) for z in range(NZ)] for x in range(2) for core in range(2)]
 
 
 def exchange(blocks, axis, groups):
     count = len(groups[0])
-    blocks = blocks.reshape(count, ROWS, 128)
-    blocks = lax.all_to_all(blocks, axis, 0, 0, axis_index_groups=groups)
-    return blocks.reshape(count * ROWS, 128)
+    moved = lax.all_to_all(blocks.reshape(count, 1, -1), axis, 0, 0, axis_index_groups=groups)
+    return moved.reshape(blocks.shape)
 
 
 def step(distribution, collision_rate):
     field = pltpu.with_memory_space_constraint(distribution.reshape(COUNT * 27, 128), pltpu.HBM)
     collision_rate = pltpu.with_memory_space_constraint(collision_rate, pltpu.HBM)
     face = (9 * COUNT, 128)
+    marked = (FACE, 128)
     whole = (27 * COUNT, 128)
     halo, column, field, rate = call(
         first_kernel,
-        [face, (NZ * ROWS, 128), whole, (1, 128)],
+        [face, (NZ * COLUMN_ROWS, 128), whole, (1, 128)],
         field,
         collision_rate,
         remote_in=2,
@@ -350,9 +352,9 @@
     )
     halo = lax.ppermute(halo, ("vel", "box"), downwind_pairs())
     column = exchange(column, "vel", COLUMNS)
-    middle, halo = call(second_kernel, [whole, face], field, rate, halo)
+    middle, halo = call(second_kernel, [whole, marked], field, rate, halo)
     halo = lax.ppermute(halo, ("vel", "box"), downwind_pairs())
-    (planes,) = call(between_kernel, [(4 * BOXES * ROWS, 128)], column, rate)
+    (planes,) = call(between_kernel, [(4 * BOXES * PLANE_ROWS, 128)], column)
     planes = exchange(planes, ("vel", "box"), PLANES)
     (out,) = call(
         third_kernel,
@@ -363,7 +365,7 @@
         planes,
         middle,
         remote_out=True,
-        scratch=[pltpu.VMEM(whole, jnp.float32), pltpu.SemaphoreType.DMA((4,))],
+        scratch=[pltpu.VMEM(whole, jnp.float32), pltpu.SemaphoreType.DMA((8,))],
     )
     return out.reshape(distribution.shape)
 

time: 59.1 us -> 47 us (0.80)
  waiting for transfers between devices: 13.6 us -> 1.88 us
  blocking collectives: 0 us -> 11.7 us
  starting transfers between devices: 39.9 us -> 28.6 us
  Pallas kernels: 5.23 us -> 4.5 us
    all_to_all x0 -> x1, blocking collectives: none -> 11.7 us  [exchange(): lax.all_to_all(blocks.reshape(count, 1, -1), axis, 0, 0, axis_index_group...]
    all_to_all x2 -> x1, starting transfers between devices: 25.1 us -> 18.3 us  [exchange(): lax.all_to_all(blocks.reshape(count, 1, -1), axis, 0, 0, axis_index_group...]
    all_to_all x2 -> x1, waiting for transfers between devices: 8.47 us -> 1.88 us  [exchange(): lax.all_to_all(blocks.reshape(count, 1, -1), axis, 0, 0, axis_index_group...]
    ppermute x2, waiting for transfers between devices: 5.11 us -> 0.01 us  [step(): halo = lax.ppermute(halo, ('vel', 'box'), downwind_pairs())]
    ppermute x2, starting transfers between devices: 14.8 us -> 10.3 us  [step(): halo = lax.ppermute(halo, ('vel', 'box'), downwind_pairs())]
    pallas_call x4, Pallas kernels: 5.23 us -> 4.5 us  [call(): pl.pallas_call(kernel, out_shape=shapes, in_specs=[hbm] * remote_in + [vm...]
  transfers between devices with their start and end apart: 4 -> 3, of which waited for: 2 -> 1; matrix products, arithmetic and copies ran while one was open for 0% -> 0% of each run, Pallas kernels for 2% -> 2%
where the time goes in v1:
time: 47 us; the launch traced here: 46.7 us
  starting transfers between devices  28.6 us (61%)
  blocking collectives  11.7 us (25%)
  Pallas kernels  4.5 us (10%)
  waiting for transfers between devices  1.88 us (4%)
    all_to_all x1, starting transfers between devices, exchange(): lax.all_to_all(blocks.reshape(count, 1, -1), axis, 0, 0, axis_index_group...  18.3 us
    all_to_all x1, blocking collectives, exchange(): lax.all_to_all(blocks.reshape(count, 1, -1), axis, 0, 0, axis_index_group...  11.7 us
    ppermute x2, starting transfers between devices, step(): halo = lax.ppermute(halo, ('vel', 'box'), downwind_pairs())  10.3 us
    pallas_call x4, Pallas kernels, call(): pl.pallas_call(kernel, out_shape=shapes, in_specs=[hbm] * remote_in + [vm...  4.5 us
    all_to_all x1, waiting for transfers between devices, exchange(): lax.all_to_all(blocks.reshape(count, 1, -1), axis, 0, 0, axis_index_group...  1.88 us
  transfers between devices with their start and end apart: 3, of which 1 were waited for; matrix products, arithmetic and copies ran while one was open for 0% of the time, Pallas kernels for 2%

profile of v1, /device:TPU:1, one launch (start us, length us, event | category | flops | bytes accessed | tf_op | source)
XLA Modules:
  0.0 46.7 jit_solution(11686968179060453880)
XLA Ops:
  0.0 2.1 %shard_map.28 = (f32[576,128]{1,0:T(8,128)S(1)}, f32[192,128]{1,0:T(8,128)}, f32[1728,128]{1,0:T(8,128)S(1)}, f32[1,128]{1,0:T(1,128)S(1)}) custom-call(f32[1728,128]{1,0:T(8,128)} %bitcast.9, f32[1,128]{1,0:T(1,128)} %rate_hbm.1), custom_call_target="tpu_custom_call" | custom-call | flops 4000000 | bytes 2163712 | tf_op jit(solution)/shard_map/pallas_call | solution.py:302
  2.1 7.9 %collective-permute-start = (f32[576,128]{1,0:T(8,128)S(1)}, f32[576,128]{1,0:T(8,128)S(1)}, u32[]{:S(2)}, u32[]{:S(2)}) collective-permute-start(f32[576,128]{1,0:T(8,128)S(1)} %get-tuple-element.13), channel_id=1, source_target_pairs={{0,7},{1,0},{2,1},{3,2},{4,3},{5,4},{6,5},{7,6},{8,15},{9,8},{10,9... | collective-permute-start | bytes 884744 | tf_op jit(solution)/shard_map/ppermute | solution.py:353
  10.0 18.3 %all-to-all-start = ((f32[16,1,1536]{2,1,0:T(1,128)}), f32[16,1,1536]{2,1,0:T(1,128)S(1)}, u32[]{:S(2)}, u32[]{:S(2)}) async-start(f32[16,1,1536]{2,1,0:T(1,128)} %bitcast.1), calls=%async_computation | async-start | bytes 196608 | tf_op jit(solution)/shard_map/all_to_all | solution.py:335
  28.3 0.0 collective-permute-done.halo
  28.3 0.7 %shard_map.29 = (f32[1728,128]{1,0:T(8,128)S(1)}, f32[584,128]{1,0:T(8,128)S(1)}) custom-call(f32[1728,128]{1,0:T(8,128)S(1)} %get-tuple-element.11.field, f32[1,128]{1,0:T(1,128)S(1)} %get-tuple-element.12.rate, f32[576,128]{1,0:T(8,128)S(1)} %collective-permute-done.halo), custom_call_target="tpu_custom_call" | custom-call | flops 4000000 | bytes 2363904 | tf_op jit(solution)/shard_map/pallas_call | solution.py:302
  29.1 2.4 %collective-permute-start.1 = (f32[584,128]{1,0:T(8,128)S(1)}, f32[584,128]{1,0:T(8,128)S(1)}, u32[]{:S(2)}, u32[]{:S(2)}) collective-permute-start(f32[584,128]{1,0:T(8,128)S(1)} %get-tuple-element.14), channel_id=1, source_target_pairs={{0,7},{1,0},{2,1},{3,2},{4,3},{5,4},{6,5},{7,6},{8,15},{9,8},{10,9... | collective-permute-start | bytes 897032 | tf_op jit(solution)/shard_map/ppermute | solution.py:356
  31.4 1.9 %all-to-all-done = f32[16,1,1536]{2,1,0:T(1,128)S(1)} async-done(((f32[16,1,1536]{2,1,0:T(1,128)}), f32[16,1,1536]{2,1,0:T(1,128)S(1)}, u32[]{:S(2)}, u32[]{:S(2)}) %all-to-all-start) | async-done | bytes 98336 | tf_op jit(solution)/shard_map/all_to_all | solution.py:335
  33.4 11.7 %all_to_all.10 = f32[32,1,1280]{2,1,0:T(1,128)S(1)} all-to-all(f32[32,1,1280]{2,1,0:T(1,128)S(1)} %bitcast.7), channel_id=1, replica_groups={{0,1,2,3,4,5,6,7,8,9,10,11,12,13,14,15,256,257,258,259,260,261,262,263,..., dimensions={0} | all-to-all | bytes 327680 | tf_op jit(solution)/shard_map/all_to_all | solution.py:335
  45.1 0.0 collective-permute-done.1.halo
  45.1 1.7 %shard_map.31 = f32[1728,128]{1,0:T(8,128)} custom-call(f32[1728,128]{1,0:T(8,128)S(1)} %get-tuple-element.11.field, f32[1,128]{1,0:T(1,128)S(1)} %get-tuple-element.12.rate, f32[584,128]{1,0:T(8,128)S(1)} %collective-permute-done.1.halo, f32[320,128]{1,0:T(8,128)S(1)} %bitcast.6, f32[1728,128]{1,0:T(8,128)S(1)} %get-tuple-element.16.middle), custom_call_target="tpu_custom_call" | custom-call | flops 4000000 | bytes 3117568 | tf_op jit(solution)/shard_map/pallas_call | solution.py:302
  (1 shorter events, 0.0 us)
Async XLA Ops:
  2.1 26.2 %collective-permute-start = (f32[576,128]{1,0:T(8,128)S(1)}, f32[576,128]{1,0:T(8,128)S(1)}, u32[]{:S(2)}, u32[]{:S(2)}) collective-permute-start(f32[576,128]{1,0:T(8,128)S(1)} %get-tuple-element.13), channel_id=1, source_target_pairs={{0,7},{1,0},{2,1},{3,2},{4,3},{5,4},{6,5},{7,6},{8,15},{9,8},{10,9... | collective-permute-start | bytes 884744 | tf_op jit(solution)/shard_map/ppermute | solution.py:353
  10.0 23.3 %all-to-all-start = ((f32[16,1,1536]{2,1,0:T(1,128)}), f32[16,1,1536]{2,1,0:T(1,128)S(1)}, u32[]{:S(2)}, u32[]{:S(2)}) async-start(f32[16,1,1536]{2,1,0:T(1,128)} %bitcast.1), calls=%async_computation | async-start | bytes 196608 | tf_op jit(solution)/shard_map/all_to_all | solution.py:335
  29.1 16.0 %collective-permute-start.1 = (f32[584,128]{1,0:T(8,128)S(1)}, f32[584,128]{1,0:T(8,128)S(1)}, u32[]{:S(2)}, u32[]{:S(2)}) collective-permute-start(f32[584,128]{1,0:T(8,128)S(1)} %get-tuple-element.14), channel_id=1, source_target_pairs={{0,7},{1,0},{2,1},{3,2},{4,3},{5,4},{6,5},{7,6},{8,15},{9,8},{10,9... | collective-permute-start | bytes 897032 | tf_op jit(solution)/shard_map/ppermute | solution.py:356

commit v2 on v1

--- a/solution.py
+++ b/solution.py
@@ -11,10 +11,12 @@
 NZ = 16
 VPD = 16
 VELS = 64
-LEAD = 8
+LEAD = 9
+PLANE_LEAD = 6
 BOXES = 8
 COUNT = 64
 STEP = 0.02
+HALF_STEP = 0.5 * STEP
 SPACING = 0.5
 FIRST = -3.75
 WEIGHT = SPACING**3
@@ -75,7 +77,7 @@
 
 def one_direction(rates, coefs, index, upper, inflow, speed, size):
     _, i1, i2 = index
-    jump = inflow - upper
+    jump = -upper if inflow is None else inflow - upper
     parts = (
         size * jump,
         (-3.0 * speed) * jump - (6.0 * size) * coefs[i1] - (6.0 * speed) * coefs[i2],
@@ -91,7 +93,7 @@
         for c in range(3):
             index = [mode(a, b, c) for a in range(3)]
             upper = trace(*(coefs[i] for i in index), place.sx)
-            one_direction(rates, coefs, index, upper, inflow_x[3 * b + c], place.wx, place.ax)
+            one_direction(rates, coefs, index, upper, inflow_x and inflow_x[3 * b + c], place.wx, place.ax)
     wy = place.wy(j)
     ay = wy * place.sy
     for a in range(3):
@@ -145,23 +147,22 @@
     return pltpu.make_async_copy(source.at[rows], target.at[rows], sems.at[j])
 
 
-def first_kernel(field_hbm, rate_hbm, halo, column, field, rate, sems):
+def first_kernel(field_hbm, rate_hbm, halo, column_hbm, field, rate, column, sems):
     place = Place()
     for j in range(4):
         chunk_copy(field_hbm, field, sems, j).start()
     rate_copy = pltpu.make_async_copy(rate_hbm, rate, sems.at[4])
     rate_copy.start()
 
-    def body(j, half, start, sums):
+    def sums_of(j, half, start, sums):
         if not half:
             chunk_copy(field_hbm, field, sems, j).wait()
-        coefs = load_coefs(field, start)
-        for k in range(9):
-            halo[pl.ds(k * COUNT + start, TILE), :] = trace(coefs[k], coefs[9 + k], coefs[18 + k], place.sx)
-        base = coefs[0]
-        out_x = place.ax * trace(base, coefs[9], coefs[18], place.sx)
-        upper_y = trace(base, coefs[3], coefs[6], place.sy)
-        upper_z = trace_z(base, coefs[1], coefs[2], half)
+        base, x1, x2, y1, y2, z1, z2 = (
+            field[pl.ds(start * 27 + m, TILE, stride=27), :] for m in (0, 9, 18, 3, 6, 1, 2)
+        )
+        out_x = place.ax * trace(base, x1, x2, place.sx)
+        upper_y = trace(base, y1, y2, place.sy)
+        upper_z = trace_z(base, z1, z2, half)
         wy = place.wy(j)
         wz = place.wz(half)
         kept = (wy * place.sy) * (place.from_y(upper_y) - upper_y) - out_x
@@ -170,11 +171,22 @@
         return tuple(s + t for s, t in zip(sums, terms))
 
     zero = jnp.zeros((TILE, 128), jnp.float32)
-    sums = lax.fori_loop(0, 4, velocity_groups(body), (zero,) * 12)
-    sums = [WEIGHT * jnp.sum(s, axis=0, keepdims=True) for s in sums]
-    for i, row in enumerate(sums):
+    sums = lax.fori_loop(0, 4, velocity_groups(sums_of), (zero,) * 12)
+    for i, s in enumerate(sums):
+        row = WEIGHT * jnp.sum(s, axis=0, keepdims=True)
         column[pl.ds(i, NZ, stride=COLUMN_ROWS), :] = jnp.broadcast_to(row, (NZ, 128))
+    column_copy = pltpu.make_async_copy(column, column_hbm, sems.at[5])
+    column_copy.start()
+
+    def traces_of(j, half, start, carry):
+        coefs = load_coefs(field, start)
+        for k in range(9):
+            halo[pl.ds(k * COUNT + start, TILE), :] = trace(coefs[k], coefs[9 + k], coefs[18 + k], place.sx)
+        return carry
+
+    lax.fori_loop(0, 4, velocity_groups(traces_of), 0)
     rate_copy.wait()
+    column_copy.wait()
 
 
 def between_kernel(column, planes):
@@ -186,7 +198,7 @@
     held, kept, gone = (all_moments(wx, rows[k : k + 4]) for k in (0, 4, 8))
     for i in range(5):
         planes[pl.ds(i, 4 * BOXES, stride=PLANE_ROWS), :] = jnp.broadcast_to(held[i], (4 * BOXES, 128))
-        box = lax.broadcasted_iota(jnp.int32, (4 * BOXES, 128), 0) % BOXES
+        box = (lax.broadcasted_iota(jnp.int32, (4 * BOXES, 128), 0) + PLANE_LEAD) % BOXES
         sent = jnp.where(box == place.box, kept[i], jnp.where(box == place.downwind, gone[i], 0.0))
         planes[pl.ds(5 + i, 4 * BOXES, stride=PLANE_ROWS), :] = sent
 
@@ -208,6 +220,22 @@
 
     lax.fori_loop(0, 4, velocity_groups(body), 0)
     halo_out[FACE - TILE :, :] = collision
+
+
+def base_kernel(field, rate, middle, base):
+    place = Place()
+    collision = jnp.broadcast_to(rate[...], (TILE, 128))
+
+    def body(j, half, start, carry):
+        coefs = [middle[pl.ds(m * COUNT + start, TILE), :] for m in range(27)]
+        rates = transport(place, coefs, None, j, half)
+        for m in range(27):
+            moved = coefs[m] + STEP * (rates[m] - collision * coefs[m])
+            old = field[pl.ds(start * 27 + m, TILE, stride=27), :]
+            base[pl.ds(m * COUNT + start, TILE), :] = 0.5 * old + 0.5 * moved
+        return carry
+
+    lax.fori_loop(0, 4, velocity_groups(body), 0)
 
 
 def states(totals):
@@ -239,10 +267,10 @@
     ]
 
 
-def third_kernel(field, rate, halo, planes, middle, out_hbm, out, sems):
+def third_kernel(rate, halo, planes, base, out_hbm, out, sems):
     place = Place()
 
-    box = lax.broadcasted_iota(jnp.int32, (4 * BOXES, 128), 0) % BOXES
+    box = (lax.broadcasted_iota(jnp.int32, (4 * BOXES, 128), 0) + PLANE_LEAD) % BOXES
     rows = [planes[pl.ds(i, 4 * BOXES, stride=PLANE_ROWS), :] for i in range(PLANE_ROWS)]
     total = lambda values: jnp.sum(values, axis=0, keepdims=True)
     totals = [total(jnp.where(box == place.box, r, 0.0)) for r in rows[:5]]
@@ -263,7 +291,9 @@
 
     now = spread_out(now, STEP * nu)
     before = spread_out(before, STEP * upwind_nu)
-    later = spread_out(later, nu)
+    later = spread_out(later, HALF_STEP * nu)
+    gain = HALF_STEP * place.ax
+    speed = HALF_STEP * place.wx
     collision = jnp.broadcast_to(nu, (TILE, 128))
 
     def body(j, half, start, carry):
@@ -276,16 +306,25 @@
             off_z = wz - flow_z
             return scale * jnp.exp((part + off_y * off_y + off_z * off_z) * inverse)
 
-        coefs = [middle[pl.ds(m * COUNT + start, TILE), :] for m in range(27)]
-        coefs[0] = coefs[0] + bell(now)
+        added = [None] * 27
+        extra = bell(now)
         inflow = [halo[pl.ds(k * COUNT + start, TILE), :] for k in range(9)]
-        inflow[0] = inflow[0] + bell(before)
-        rates = transport(place, coefs, inflow, j, half)
-        rates[0] = rates[0] + bell(later)
+        inflow[0] = inflow[0] + bell(before) - extra
+        for k in range(9):
+            added[k] = gain * inflow[k]
+            added[9 + k] = (-3.0 * speed) * inflow[k]
+            added[18 + k] = (5.0 * gain) * inflow[k]
+        added[0] = added[0] + (0.5 - HALF_STEP * collision) * extra + bell(later)
+        lines = (
+            (HALF_STEP * wy, HALF_STEP * (wy * place.sy), place.from_y(extra) - extra, 3),
+            (HALF_STEP * wz, HALF_STEP * (wz if half else -wz), place.from_z(extra, half) - extra, 1),
+        )
+        for line, size, jump, i in lines:
+            added[0] = added[0] + size * jump
+            added[i] = added[i] - (3.0 * line) * jump
+            added[2 * i] = added[2 * i] + (5.0 * size) * jump
         for m in range(27):
-            here = pl.ds(start * 27 + m, TILE, stride=27)
-            moved = coefs[m] + STEP * (rates[m] - collision * coefs[m])
-            out[here, :] = 0.5 * field[here, :] + 0.5 * moved
+            out[pl.ds(start * 27 + m, TILE, stride=27), :] = base[pl.ds(m * COUNT + start, TILE), :] + added[m]
         chunk_copy(out, out_hbm, sems, 2 * j + half, CHUNK // 2).start()
         return carry
 
@@ -294,7 +333,7 @@
         chunk_copy(out, out_hbm, sems, j, CHUNK // 2).wait()
 
 
-def call(kernel, outs, *args, remote_in=0, remote_out=False, scratch=()):
+def call(kernel, outs, *args, remote_in=0, remote_out=(), scratch=()):
     vmem = pl.BlockSpec(memory_space=pltpu.VMEM)
     hbm = pl.BlockSpec(memory_space=pltpu.HBM)
     shapes = [jax.ShapeDtypeStruct(s, jnp.float32) for s in outs]
@@ -303,7 +342,7 @@
         kernel,
         out_shape=shapes,
         in_specs=[hbm] * remote_in + [vmem] * (len(args) - remote_in),
-        out_specs=[hbm if remote_out else vmem] * len(outs),
+        out_specs=[hbm if i in remote_out else vmem for i in range(len(outs))],
         scratch_shapes=scratch,
         compiler_params=pltpu.CompilerParams(vmem_limit_bytes=GRANT),
         cost_estimate=pl.CostEstimate(flops=4000000, bytes_accessed=moved, transcendentals=30000),
@@ -327,6 +366,7 @@
     [vel_of(x, z, core) * BOXES + box for x in range(2) for core in range(2) for box in range(BOXES)]
     for z in range(NZ)
 ]
+PLANES = [group[PLANE_LEAD:] + group[:PLANE_LEAD] for group in PLANES]
 COLUMNS = [[vel_of(x, (z + LEAD) % NZ, core) for z in range(NZ)] for x in range(2) for core in range(2)]
 
 
@@ -348,23 +388,24 @@
         field,
         collision_rate,
         remote_in=2,
-        scratch=[pltpu.SemaphoreType.DMA((5,))],
+        remote_out=(1,),
+        scratch=[pltpu.VMEM((NZ * COLUMN_ROWS, 128), jnp.float32), pltpu.SemaphoreType.DMA((6,))],
     )
     halo = lax.ppermute(halo, ("vel", "box"), downwind_pairs())
     column = exchange(column, "vel", COLUMNS)
     middle, halo = call(second_kernel, [whole, marked], field, rate, halo)
     halo = lax.ppermute(halo, ("vel", "box"), downwind_pairs())
+    (base,) = call(base_kernel, [whole], field, rate, middle)
     (planes,) = call(between_kernel, [(4 * BOXES * PLANE_ROWS, 128)], column)
     planes = exchange(planes, ("vel", "box"), PLANES)
     (out,) = call(
         third_kernel,
         [whole],
-        field,
         rate,
         halo,
         planes,
-        middle,
-        remote_out=True,
+        base,
+        remote_out=(0,),
         scratch=[pltpu.VMEM(whole, jnp.float32), pltpu.SemaphoreType.DMA((8,))],
     )
     return out.reshape(distribution.shape)

time: 47 us -> 47 us (level)
  blocking collectives: 11.7 us -> 0 us
  starting transfers between devices: 28.6 us -> 36.3 us
  waiting for transfers between devices: 1.88 us -> 4.74 us
  Pallas kernels: 4.5 us -> 5.61 us
    all_to_all x1 -> x0, blocking collectives: 11.7 us -> none  [exchange(): lax.all_to_all(blocks.reshape(count, 1, -1), axis, 0, 0, axis_index_group...]
    all_to_all x1 -> x2, starting transfers between devices: 18.3 us -> 26 us  [exchange(): lax.all_to_all(blocks.reshape(count, 1, -1), axis, 0, 0, axis_index_group...]
    all_to_all x1 -> x2, waiting for transfers between devices: 1.88 us -> 4.73 us  [exchange(): lax.all_to_all(blocks.reshape(count, 1, -1), axis, 0, 0, axis_index_group...]
    pallas_call x4 -> x5, Pallas kernels: 4.5 us -> 5.61 us  [call(): pl.pallas_call(kernel, out_shape=shapes, in_specs=[hbm] * remote_in + [vm...]
  transfers between devices with their start and end apart: 3 -> 4, of which waited for: 1 -> 2; matrix products, arithmetic and copies ran while one was open for 0% -> 0% of each run, Pallas kernels for 2% -> 5%
where the time goes in v2:
time: 47 us; the launch traced here: 46.7 us
  starting transfers between devices  36.3 us (77%)
  Pallas kernels  5.61 us (12%)
  waiting for transfers between devices  4.74 us (10%)
    all_to_all x2, starting transfers between devices, exchange(): lax.all_to_all(blocks.reshape(count, 1, -1), axis, 0, 0, axis_index_group...  26 us
    ppermute x2, starting transfers between devices, step(): halo = lax.ppermute(halo, ('vel', 'box'), downwind_pairs())  10.3 us
    pallas_call x5, Pallas kernels, call(): pl.pallas_call(kernel, out_shape=shapes, in_specs=[hbm] * remote_in + [vm...  5.61 us
    all_to_all x2, waiting for transfers between devices, exchange(): lax.all_to_all(blocks.reshape(count, 1, -1), axis, 0, 0, axis_index_group...  4.73 us
  transfers between devices with their start and end apart: 4, of which 2 were waited for; matrix products, arithmetic and copies ran while one was open for 0% of the time, Pallas kernels for 5%

profile of v2, /device:TPU:1, one launch (start us, length us, event | category | flops | bytes accessed | tf_op | source)
XLA Modules:
  0.0 46.7 jit_solution(8517547792546614913)
XLA Ops:
  0.0 2.1 %shard_map.28 = (f32[576,128]{1,0:T(8,128)S(1)}, f32[192,128]{1,0:T(8,128)}, f32[1728,128]{1,0:T(8,128)S(1)}, f32[1,128]{1,0:T(1,128)S(1)}) custom-call(f32[1728,128]{1,0:T(8,128)} %bitcast.8, f32[1,128]{1,0:T(1,128)} %rate_hbm.1), custom_call_target="tpu_custom_call" | custom-call | flops 4000000 | bytes 2163712 | tf_op jit(solution)/shard_map/pallas_call | solution.py:341
  2.1 7.9 %collective-permute-start = (f32[576,128]{1,0:T(8,128)S(1)}, f32[576,128]{1,0:T(8,128)S(1)}, u32[]{:S(2)}, u32[]{:S(2)}) collective-permute-start(f32[576,128]{1,0:T(8,128)S(1)} %get-tuple-element.13), channel_id=1, source_target_pairs={{0,7},{1,0},{2,1},{3,2},{4,3},{5,4},{6,5},{7,6},{8,15},{9,8},{10,9... | collective-permute-start | bytes 884744 | tf_op jit(solution)/shard_map/ppermute | solution.py:394
  10.0 17.4 %all-to-all-start = ((f32[16,1,1536]{2,1,0:T(1,128)}), f32[16,1,1536]{2,1,0:T(1,128)S(1)}, u32[]{:S(2)}, u32[]{:S(2)}) async-start(f32[16,1,1536]{2,1,0:T(1,128)} %bitcast.1), calls=%async_computation | async-start | bytes 196608 | tf_op jit(solution)/shard_map/all_to_all | solution.py:375
  27.4 0.0 collective-permute-done.halo
  27.4 0.7 %shard_map.29 = (f32[1728,128]{1,0:T(8,128)S(1)}, f32[584,128]{1,0:T(8,128)S(1)}) custom-call(f32[1728,128]{1,0:T(8,128)S(1)} %get-tuple-element.12.field, f32[1,128]{1,0:T(1,128)S(1)} %get-tuple-element.11.rate, f32[576,128]{1,0:T(8,128)S(1)} %collective-permute-done.halo), custom_call_target="tpu_custom_call" | custom-call | flops 4000000 | bytes 2363904 | tf_op jit(solution)/shard_map/pallas_call | solution.py:341
  28.2 2.4 %collective-permute-start.1 = (f32[584,128]{1,0:T(8,128)S(1)}, f32[584,128]{1,0:T(8,128)S(1)}, u32[]{:S(2)}, u32[]{:S(2)}) collective-permute-start(f32[584,128]{1,0:T(8,128)S(1)} %get-tuple-element.14), channel_id=1, source_target_pairs={{0,7},{1,0},{2,1},{3,2},{4,3},{5,4},{6,5},{7,6},{8,15},{9,8},{10,9... | collective-permute-start | bytes 897032 | tf_op jit(solution)/shard_map/ppermute | solution.py:397
  30.5 2.4 %all-to-all-done = f32[16,1,1536]{2,1,0:T(1,128)S(1)} async-done(((f32[16,1,1536]{2,1,0:T(1,128)}), f32[16,1,1536]{2,1,0:T(1,128)S(1)}, u32[]{:S(2)}, u32[]{:S(2)}) %all-to-all-start) | async-done | bytes 98336 | tf_op jit(solution)/shard_map/all_to_all | solution.py:375
  33.0 0.7 %shard_map.30 = f32[320,128]{1,0:T(8,128)} custom-call(f32[192,128]{1,0:T(8,128)S(1)} %bitcast.7), custom_call_target="tpu_custom_call" | custom-call | flops 4000000 | bytes 262144 | tf_op jit(solution)/shard_map/pallas_call | solution.py:341
  33.7 8.6 %all-to-all-start.1 = ((f32[32,1,1280]{2,1,0:T(1,128)}), f32[32,1,1280]{2,1,0:T(1,128)S(1)}, u32[]{:S(2)}, u32[]{:S(2)}) async-start(f32[32,1,1280]{2,1,0:T(1,128)} %bitcast.3), calls=%async_computation.1 | async-start | bytes 327680 | tf_op jit(solution)/shard_map/all_to_all | solution.py:375
  42.3 0.8 %shard_map.31.base = f32[1728,128]{1,0:T(8,128)S(1)} custom-call(f32[1728,128]{1,0:T(8,128)S(1)} %get-tuple-element.12.field, f32[1,128]{1,0:T(1,128)S(1)} %get-tuple-element.11.rate, f32[1728,128]{1,0:T(8,128)S(1)} %get-tuple-element.16.middle), custom_call_target="tpu_custom_call" | custom-call | flops 4000000 | bytes 2654720 | tf_op jit(solution)/shard_map/pallas_call | solution.py:341
  43.2 2.3 %all-to-all-done.1 = f32[32,1,1280]{2,1,0:T(1,128)S(1)} async-done(((f32[32,1,1280]{2,1,0:T(1,128)}), f32[32,1,1280]{2,1,0:T(1,128)S(1)}, u32[]{:S(2)}, u32[]{:S(2)}) %all-to-all-start.1) | async-done | bytes 163872 | tf_op jit(solution)/shard_map/all_to_all | solution.py:375
  45.5 0.0 collective-permute-done.1.halo
  45.5 1.3 %shard_map.32 = f32[1728,128]{1,0:T(8,128)} custom-call(f32[1,128]{1,0:T(1,128)S(1)} %get-tuple-element.11.rate, f32[584,128]{1,0:T(8,128)S(1)} %collective-permute-done.1.halo, f32[320,128]{1,0:T(8,128)S(1)} %bitcast.6, f32[1728,128]{1,0:T(8,128)S(1)} %shard_map.31.base), custom_call_target="tpu_custom_call" | custom-call | flops 4000000 | bytes 2232832 | tf_op jit(solution)/shard_map/pallas_call | solution.py:341
Async XLA Ops:
  2.1 25.3 %collective-permute-start = (f32[576,128]{1,0:T(8,128)S(1)}, f32[576,128]{1,0:T(8,128)S(1)}, u32[]{:S(2)}, u32[]{:S(2)}) collective-permute-start(f32[576,128]{1,0:T(8,128)S(1)} %get-tuple-element.13), channel_id=1, source_target_pairs={{0,7},{1,0},{2,1},{3,2},{4,3},{5,4},{6,5},{7,6},{8,15},{9,8},{10,9... | collective-permute-start | bytes 884744 | tf_op jit(solution)/shard_map/ppermute | solution.py:394
  10.0 23.0 %all-to-all-start = ((f32[16,1,1536]{2,1,0:T(1,128)}), f32[16,1,1536]{2,1,0:T(1,128)S(1)}, u32[]{:S(2)}, u32[]{:S(2)}) async-start(f32[16,1,1536]{2,1,0:T(1,128)} %bitcast.1), calls=%async_computation | async-start | bytes 196608 | tf_op jit(solution)/shard_map/all_to_all | solution.py:375
  28.2 17.3 %collective-permute-start.1 = (f32[584,128]{1,0:T(8,128)S(1)}, f32[584,128]{1,0:T(8,128)S(1)}, u32[]{:S(2)}, u32[]{:S(2)}) collective-permute-start(f32[584,128]{1,0:T(8,128)S(1)} %get-tuple-element.14), channel_id=1, source_target_pairs={{0,7},{1,0},{2,1},{3,2},{4,3},{5,4},{6,5},{7,6},{8,15},{9,8},{10,9... | collective-permute-start | bytes 897032 | tf_op jit(solution)/shard_map/ppermute | solution.py:397
  33.7 11.8 %all-to-all-start.1 = ((f32[32,1,1280]{2,1,0:T(1,128)}), f32[32,1,1280]{2,1,0:T(1,128)S(1)}, u32[]{:S(2)}, u32[]{:S(2)}) async-start(f32[32,1,1280]{2,1,0:T(1,128)} %bitcast.3), calls=%async_computation.1 | async-start | bytes 327680 | tf_op jit(solution)/shard_map/all_to_all | solution.py:375

commit v3 on v2

--- a/solution.py
+++ b/solution.py
@@ -11,8 +11,8 @@
 NZ = 16
 VPD = 16
 VELS = 64
-LEAD = 9
-PLANE_LEAD = 6
+LEAD = 10
+PLANE_LEAD = 14
 BOXES = 8
 COUNT = 64
 STEP = 0.02
@@ -50,6 +50,7 @@
         self.shift_y = jnp.where(up, NZ, 128 - NZ)
         self.upwind = jnp.where(right, (self.box + BOXES - 1) % BOXES, (self.box + 1) % BOXES)
         self.downwind = jnp.where(right, (self.box + 1) % BOXES, (self.box + BOXES - 1) % BOXES)
+        self.waits = jnp.logical_not(right) & (self.box % (BOXES // 2) == 0)
         self.lane = lax.broadcasted_iota(jnp.int32, (TILE, 128), 1) % NZ
 
     def wy(self, j):
@@ -147,16 +148,8 @@
     return pltpu.make_async_copy(source.at[rows], target.at[rows], sems.at[j])
 
 
-def first_kernel(field_hbm, rate_hbm, halo, column_hbm, field, rate, column, sems):
-    place = Place()
-    for j in range(4):
-        chunk_copy(field_hbm, field, sems, j).start()
-    rate_copy = pltpu.make_async_copy(rate_hbm, rate, sems.at[4])
-    rate_copy.start()
-
+def send_moments(place, field, column, column_hbm, sem):
     def sums_of(j, half, start, sums):
-        if not half:
-            chunk_copy(field_hbm, field, sems, j).wait()
         base, x1, x2, y1, y2, z1, z2 = (
             field[pl.ds(start * 27 + m, TILE, stride=27), :] for m in (0, 9, 18, 3, 6, 1, 2)
         )
@@ -175,10 +168,21 @@
     for i, s in enumerate(sums):
         row = WEIGHT * jnp.sum(s, axis=0, keepdims=True)
         column[pl.ds(i, NZ, stride=COLUMN_ROWS), :] = jnp.broadcast_to(row, (NZ, 128))
-    column_copy = pltpu.make_async_copy(column, column_hbm, sems.at[5])
-    column_copy.start()
+    copy = pltpu.make_async_copy(column, column_hbm, sem)
+    copy.start()
+    copy.wait()
+
+
+def first_kernel(field_hbm, rate_hbm, halo, column_hbm, field, rate, column, sems):
+    place = Place()
+    for j in range(4):
+        chunk_copy(field_hbm, field, sems, j).start()
+    rate_copy = pltpu.make_async_copy(rate_hbm, rate, sems.at[4])
+    rate_copy.start()
 
     def traces_of(j, half, start, carry):
+        if not half:
+            chunk_copy(field_hbm, field, sems, j).wait()
         coefs = load_coefs(field, start)
         for k in range(9):
             halo[pl.ds(k * COUNT + start, TILE), :] = trace(coefs[k], coefs[9 + k], coefs[18 + k], place.sx)
@@ -186,7 +190,18 @@
 
     lax.fori_loop(0, 4, velocity_groups(traces_of), 0)
     rate_copy.wait()
-    column_copy.wait()
+
+    @pl.when(place.waits)
+    def _():
+        send_moments(place, field, column, column_hbm, sems.at[5])
+
+
+def moments_kernel(field, _, column_hbm, column, sems):
+    place = Place()
+
+    @pl.when(jnp.logical_not(place.waits))
+    def _():
+        send_moments(place, field, column, column_hbm, sems.at[0])
 
 
 def between_kernel(column, planes):
@@ -333,7 +348,7 @@
         chunk_copy(out, out_hbm, sems, j, CHUNK // 2).wait()
 
 
-def call(kernel, outs, *args, remote_in=0, remote_out=(), scratch=()):
+def call(kernel, outs, *args, remote_in=(), remote_out=(), scratch=(), aliases=None):
     vmem = pl.BlockSpec(memory_space=pltpu.VMEM)
     hbm = pl.BlockSpec(memory_space=pltpu.HBM)
     shapes = [jax.ShapeDtypeStruct(s, jnp.float32) for s in outs]
@@ -341,9 +356,10 @@
     return pl.pallas_call(
         kernel,
         out_shape=shapes,
-        in_specs=[hbm] * remote_in + [vmem] * (len(args) - remote_in),
+        in_specs=[hbm if i in remote_in else vmem for i in range(len(args))],
         out_specs=[hbm if i in remote_out else vmem for i in range(len(outs))],
         scratch_shapes=scratch,
+        input_output_aliases=aliases or {},
         compiler_params=pltpu.CompilerParams(vmem_limit_bytes=GRANT),
         cost_estimate=pl.CostEstimate(flops=4000000, bytes_accessed=moved, transcendentals=30000),
     )(*args)
@@ -387,11 +403,21 @@
         [face, (NZ * COLUMN_ROWS, 128), whole, (1, 128)],
         field,
         collision_rate,
-        remote_in=2,
+        remote_in=(0, 1),
         remote_out=(1,),
         scratch=[pltpu.VMEM((NZ * COLUMN_ROWS, 128), jnp.float32), pltpu.SemaphoreType.DMA((6,))],
     )
     halo = lax.ppermute(halo, ("vel", "box"), downwind_pairs())
+    (column,) = call(
+        moments_kernel,
+        [(NZ * COLUMN_ROWS, 128)],
+        field,
+        column,
+        remote_in=(1,),
+        remote_out=(0,),
+        scratch=[pltpu.VMEM((NZ * COLUMN_ROWS, 128), jnp.float32), pltpu.SemaphoreType.DMA((1,))],
+        aliases={1: 0},
+    )
     column = exchange(column, "vel", COLUMNS)
     middle, halo = call(second_kernel, [whole, marked], field, rate, halo)
     halo = lax.ppermute(halo, ("vel", "box"), downwind_pairs())

time: 47 us -> 46.1 us (0.981)
  starting transfers between devices: 36.3 us -> 35.5 us
  waiting for transfers between devices: 4.74 us -> 4.26 us
    all_to_all x2, starting transfers between devices: 26 us -> 25.3 us  [exchange(): lax.all_to_all(blocks.reshape(count, 1, -1), axis, 0, 0, axis_index_group...]
    all_to_all x2, waiting for transfers between devices: 4.73 us -> 4.26 us  [exchange(): lax.all_to_all(blocks.reshape(count, 1, -1), axis, 0, 0, axis_index_group...]
    pallas_call x5 -> x6, Pallas kernels: 5.61 us -> 5.91 us  [call(): pl.pallas_call(kernel, out_shape=shapes, in_specs=[hbm if i in remote_in...]
where the time goes in v3:
time: 46.1 us; the launch traced here: 45.8 us
  starting transfers between devices  35.5 us (77%)
  Pallas kernels  5.91 us (13%)
  waiting for transfers between devices  4.26 us (9%)
    all_to_all x2, starting transfers between devices, exchange(): lax.all_to_all(blocks.reshape(count, 1, -1), axis, 0, 0, axis_index_group...  25.3 us
    ppermute x2, starting transfers between devices, step(): halo = lax.ppermute(halo, ('vel', 'box'), downwind_pairs())  10.3 us
    pallas_call x6, Pallas kernels, call(): pl.pallas_call(kernel, out_shape=shapes, in_specs=[hbm if i in remote_in...  5.91 us
    all_to_all x2, waiting for transfers between devices, exchange(): lax.all_to_all(blocks.reshape(count, 1, -1), axis, 0, 0, axis_index_group...  4.26 us
  transfers between devices with their start and end apart: 4, of which 2 were waited for; matrix products, arithmetic and copies ran while one was open for 0% of the time, Pallas kernels for 5%

profile of v3, /device:TPU:1, one launch (start us, length us, event | category | flops | bytes accessed | tf_op | source)
XLA Modules:
  0.0 45.8 jit_solution(3355623974187896795)
XLA Ops:
  0.0 2.3 %shard_map.28 = (f32[576,128]{1,0:T(8,128)S(1)}, f32[192,128]{1,0:T(8,128)}, f32[1728,128]{1,0:T(8,128)S(1)}, f32[1,128]{1,0:T(1,128)S(1)}) custom-call(f32[1728,128]{1,0:T(8,128)} %bitcast.8, f32[1,128]{1,0:T(1,128)} %rate_hbm.1), custom_call_target="tpu_custom_call" | custom-call | flops 4000000 | bytes 2163712 | tf_op jit(solution)/shard_map/pallas_call | solution.py:356
  2.3 6.9 %collective-permute-start = (f32[576,128]{1,0:T(8,128)S(1)}, f32[576,128]{1,0:T(8,128)S(1)}, u32[]{:S(2)}, u32[]{:S(2)}) collective-permute-start(f32[576,128]{1,0:T(8,128)S(1)} %get-tuple-element.13), channel_id=1, source_target_pairs={{0,7},{1,0},{2,1},{3,2},{4,3},{5,4},{6,5},{7,6},{8,15},{9,8},{10,9... | collective-permute-start | bytes 884744 | tf_op jit(solution)/shard_map/ppermute | solution.py:410
  9.3 16.5 %all-to-all-start = ((f32[16,1,1536]{2,1,0:T(1,128)}), f32[16,1,1536]{2,1,0:T(1,128)S(1)}, u32[]{:S(2)}, u32[]{:S(2)}) async-start(f32[16,1,1536]{2,1,0:T(1,128)} %bitcast.1), calls=%async_computation | async-start | bytes 196608 | tf_op jit(solution)/shard_map/all_to_all | solution.py:391
  25.8 0.0 collective-permute-done.halo
  25.8 0.7 %shard_map.29 = (f32[1728,128]{1,0:T(8,128)S(1)}, f32[584,128]{1,0:T(8,128)S(1)}) custom-call(f32[1728,128]{1,0:T(8,128)S(1)} %get-tuple-element.12.field, f32[1,128]{1,0:T(1,128)S(1)} %get-tuple-element.11.rate, f32[576,128]{1,0:T(8,128)S(1)} %collective-permute-done.halo), custom_call_target="tpu_custom_call" | custom-call | flops 4000000 | bytes 2363904 | tf_op jit(solution)/shard_map/pallas_call | solution.py:356
  26.6 3.4 %collective-permute-start.1 = (f32[584,128]{1,0:T(8,128)S(1)}, f32[584,128]{1,0:T(8,128)S(1)}, u32[]{:S(2)}, u32[]{:S(2)}) collective-permute-start(f32[584,128]{1,0:T(8,128)S(1)} %get-tuple-element.14), channel_id=1, source_target_pairs={{0,7},{1,0},{2,1},{3,2},{4,3},{5,4},{6,5},{7,6},{8,15},{9,8},{10,9... | collective-permute-start | bytes 897032 | tf_op jit(solution)/shard_map/ppermute | solution.py:423
  29.9 1.9 %all-to-all-done = f32[16,1,1536]{2,1,0:T(1,128)S(1)} async-done(((f32[16,1,1536]{2,1,0:T(1,128)}), f32[16,1,1536]{2,1,0:T(1,128)S(1)}, u32[]{:S(2)}, u32[]{:S(2)}) %all-to-all-start) | async-done | bytes 98336 | tf_op jit(solution)/shard_map/all_to_all | solution.py:391
  31.9 0.7 %shard_map.31 = f32[320,128]{1,0:T(8,128)} custom-call(f32[192,128]{1,0:T(8,128)S(1)} %bitcast.7), custom_call_target="tpu_custom_call" | custom-call | flops 4000000 | bytes 262144 | tf_op jit(solution)/shard_map/pallas_call | solution.py:356
  32.6 8.8 %all-to-all-start.1 = ((f32[32,1,1280]{2,1,0:T(1,128)}), f32[32,1,1280]{2,1,0:T(1,128)S(1)}, u32[]{:S(2)}, u32[]{:S(2)}) async-start(f32[32,1,1280]{2,1,0:T(1,128)} %bitcast.3), calls=%async_computation.1 | async-start | bytes 327680 | tf_op jit(solution)/shard_map/all_to_all | solution.py:391
  41.4 0.8 %shard_map.32.base = f32[1728,128]{1,0:T(8,128)S(1)} custom-call(f32[1728,128]{1,0:T(8,128)S(1)} %get-tuple-element.12.field, f32[1,128]{1,0:T(1,128)S(1)} %get-tuple-element.11.rate, f32[1728,128]{1,0:T(8,128)S(1)} %get-tuple-element.16.middle), custom_call_target="tpu_custom_call" | custom-call | flops 4000000 | bytes 2654720 | tf_op jit(solution)/shard_map/pallas_call | solution.py:356
  42.2 2.3 %all-to-all-done.1 = f32[32,1,1280]{2,1,0:T(1,128)S(1)} async-done(((f32[32,1,1280]{2,1,0:T(1,128)}), f32[32,1,1280]{2,1,0:T(1,128)S(1)}, u32[]{:S(2)}, u32[]{:S(2)}) %all-to-all-start.1) | async-done | bytes 163872 | tf_op jit(solution)/shard_map/all_to_all | solution.py:391
  44.5 0.0 collective-permute-done.1.halo
  44.5 1.3 %shard_map.33 = f32[1728,128]{1,0:T(8,128)} custom-call(f32[1,128]{1,0:T(1,128)S(1)} %get-tuple-element.11.rate, f32[584,128]{1,0:T(8,128)S(1)} %collective-permute-done.1.halo, f32[320,128]{1,0:T(8,128)S(1)} %bitcast.6, f32[1728,128]{1,0:T(8,128)S(1)} %shard_map.32.base), custom_call_target="tpu_custom_call" | custom-call | flops 4000000 | bytes 2232832 | tf_op jit(solution)/shard_map/pallas_call | solution.py:356
  (1 shorter events, 0.0 us)
Async XLA Ops:
  2.3 23.5 %collective-permute-start = (f32[576,128]{1,0:T(8,128)S(1)}, f32[576,128]{1,0:T(8,128)S(1)}, u32[]{:S(2)}, u32[]{:S(2)}) collective-permute-start(f32[576,128]{1,0:T(8,128)S(1)} %get-tuple-element.13), channel_id=1, source_target_pairs={{0,7},{1,0},{2,1},{3,2},{4,3},{5,4},{6,5},{7,6},{8,15},{9,8},{10,9... | collective-permute-start | bytes 884744 | tf_op jit(solution)/shard_map/ppermute | solution.py:410
  9.3 22.6 %all-to-all-start = ((f32[16,1,1536]{2,1,0:T(1,128)}), f32[16,1,1536]{2,1,0:T(1,128)S(1)}, u32[]{:S(2)}, u32[]{:S(2)}) async-start(f32[16,1,1536]{2,1,0:T(1,128)} %bitcast.1), calls=%async_computation | async-start | bytes 196608 | tf_op jit(solution)/shard_map/all_to_all | solution.py:391
  26.6 17.9 %collective-permute-start.1 = (f32[584,128]{1,0:T(8,128)S(1)}, f32[584,128]{1,0:T(8,128)S(1)}, u32[]{:S(2)}, u32[]{:S(2)}) collective-permute-start(f32[584,128]{1,0:T(8,128)S(1)} %get-tuple-element.14), channel_id=1, source_target_pairs={{0,7},{1,0},{2,1},{3,2},{4,3},{5,4},{6,5},{7,6},{8,15},{9,8},{10,9... | collective-permute-start | bytes 897032 | tf_op jit(solution)/shard_map/ppermute | solution.py:423
  32.6 11.9 %all-to-all-start.1 = ((f32[32,1,1280]{2,1,0:T(1,128)}), f32[32,1,1280]{2,1,0:T(1,128)S(1)}, u32[]{:S(2)}, u32[]{:S(2)}) async-start(f32[32,1,1280]{2,1,0:T(1,128)} %bitcast.3), calls=%async_computation.1 | async-start | bytes 327680 | tf_op jit(solution)/shard_map/all_to_all | solution.py:391

commit v4 on v3

--- a/solution.py
+++ b/solution.py
@@ -143,8 +143,8 @@
     ]
 
 
-def chunk_copy(source, target, sems, j, size=CHUNK):
-    rows = pl.ds(pl.multiple_of(j * size, size), size)
+def chunk_copy(source, target, sems, j):
+    rows = pl.ds(pl.multiple_of(j * CHUNK, CHUNK), CHUNK)
     return pltpu.make_async_copy(source.at[rows], target.at[rows], sems.at[j])
 
 
@@ -340,12 +340,13 @@
             added[2 * i] = added[2 * i] + (5.0 * size) * jump
         for m in range(27):
             out[pl.ds(start * 27 + m, TILE, stride=27), :] = base[pl.ds(m * COUNT + start, TILE), :] + added[m]
-        chunk_copy(out, out_hbm, sems, 2 * j + half, CHUNK // 2).start()
+        if half:
+            chunk_copy(out, out_hbm, sems, j).start()
         return carry
 
     lax.fori_loop(0, 4, velocity_groups(body), 0)
-    for j in range(8):
-        chunk_copy(out, out_hbm, sems, j, CHUNK // 2).wait()
+    for j in range(4):
+        chunk_copy(out, out_hbm, sems, j).wait()
 
 
 def call(kernel, outs, *args, remote_in=(), remote_out=(), scratch=(), aliases=None):
@@ -432,7 +433,7 @@
         planes,
         base,
         remote_out=(0,),
-        scratch=[pltpu.VMEM(whole, jnp.float32), pltpu.SemaphoreType.DMA((8,))],
+        scratch=[pltpu.VMEM(whole, jnp.float32), pltpu.SemaphoreType.DMA((4,))],
     )
     return out.reshape(distribution.shape)
 

time: 46.1 us -> 46 us (level)
  no operation moved by 1% of the time
where the time goes in v4:
time: 46 us; the launch traced here: 45.7 us
  starting transfers between devices  35.5 us (77%)
  Pallas kernels  5.86 us (13%)
  waiting for transfers between devices  4.26 us (9%)
    all_to_all x2, starting transfers between devices, exchange(): lax.all_to_all(blocks.reshape(count, 1, -1), axis, 0, 0, axis_index_group...  25.3 us
    ppermute x2, starting transfers between devices, step(): halo = lax.ppermute(halo, ('vel', 'box'), downwind_pairs())  10.3 us
    pallas_call x6, Pallas kernels, call(): pl.pallas_call(kernel, out_shape=shapes, in_specs=[hbm if i in remote_in...  5.86 us
    all_to_all x2, waiting for transfers between devices, exchange(): lax.all_to_all(blocks.reshape(count, 1, -1), axis, 0, 0, axis_index_group...  4.26 us
  transfers between devices with their start and end apart: 4, of which 2 were waited for; matrix products, arithmetic and copies ran while one was open for 0% of the time, Pallas kernels for 5%

profile of v4, /device:TPU:1, one launch (start us, length us, event | category | flops | bytes accessed | tf_op | source)
XLA Modules:
  0.0 45.7 jit_solution(18238388307643712995)
XLA Ops:
  0.0 2.3 %shard_map.28 = (f32[576,128]{1,0:T(8,128)S(1)}, f32[192,128]{1,0:T(8,128)}, f32[1728,128]{1,0:T(8,128)S(1)}, f32[1,128]{1,0:T(1,128)S(1)}) custom-call(f32[1728,128]{1,0:T(8,128)} %bitcast.8, f32[1,128]{1,0:T(1,128)} %rate_hbm.1), custom_call_target="tpu_custom_call" | custom-call | flops 4000000 | bytes 2163712 | tf_op jit(solution)/shard_map/pallas_call | solution.py:357
  2.3 6.9 %collective-permute-start = (f32[576,128]{1,0:T(8,128)S(1)}, f32[576,128]{1,0:T(8,128)S(1)}, u32[]{:S(2)}, u32[]{:S(2)}) collective-permute-start(f32[576,128]{1,0:T(8,128)S(1)} %get-tuple-element.13), channel_id=1, source_target_pairs={{0,7},{1,0},{2,1},{3,2},{4,3},{5,4},{6,5},{7,6},{8,15},{9,8},{10,9... | collective-permute-start | bytes 884744 | tf_op jit(solution)/shard_map/ppermute | solution.py:411
  9.3 16.5 %all-to-all-start = ((f32[16,1,1536]{2,1,0:T(1,128)}), f32[16,1,1536]{2,1,0:T(1,128)S(1)}, u32[]{:S(2)}, u32[]{:S(2)}) async-start(f32[16,1,1536]{2,1,0:T(1,128)} %bitcast.1), calls=%async_computation | async-start | bytes 196608 | tf_op jit(solution)/shard_map/all_to_all | solution.py:392
  25.8 0.0 collective-permute-done.halo
  25.8 0.7 %shard_map.29 = (f32[1728,128]{1,0:T(8,128)S(1)}, f32[584,128]{1,0:T(8,128)S(1)}) custom-call(f32[1728,128]{1,0:T(8,128)S(1)} %get-tuple-element.12.field, f32[1,128]{1,0:T(1,128)S(1)} %get-tuple-element.11.rate, f32[576,128]{1,0:T(8,128)S(1)} %collective-permute-done.halo), custom_call_target="tpu_custom_call" | custom-call | flops 4000000 | bytes 2363904 | tf_op jit(solution)/shard_map/pallas_call | solution.py:357
  26.6 3.4 %collective-permute-start.1 = (f32[584,128]{1,0:T(8,128)S(1)}, f32[584,128]{1,0:T(8,128)S(1)}, u32[]{:S(2)}, u32[]{:S(2)}) collective-permute-start(f32[584,128]{1,0:T(8,128)S(1)} %get-tuple-element.14), channel_id=1, source_target_pairs={{0,7},{1,0},{2,1},{3,2},{4,3},{5,4},{6,5},{7,6},{8,15},{9,8},{10,9... | collective-permute-start | bytes 897032 | tf_op jit(solution)/shard_map/ppermute | solution.py:424
  29.9 1.9 %all-to-all-done = f32[16,1,1536]{2,1,0:T(1,128)S(1)} async-done(((f32[16,1,1536]{2,1,0:T(1,128)}), f32[16,1,1536]{2,1,0:T(1,128)S(1)}, u32[]{:S(2)}, u32[]{:S(2)}) %all-to-all-start) | async-done | bytes 98336 | tf_op jit(solution)/shard_map/all_to_all | solution.py:392
  31.9 0.7 %shard_map.31 = f32[320,128]{1,0:T(8,128)} custom-call(f32[192,128]{1,0:T(8,128)S(1)} %bitcast.7), custom_call_target="tpu_custom_call" | custom-call | flops 4000000 | bytes 262144 | tf_op jit(solution)/shard_map/pallas_call | solution.py:357
  32.6 8.8 %all-to-all-start.1 = ((f32[32,1,1280]{2,1,0:T(1,128)}), f32[32,1,1280]{2,1,0:T(1,128)S(1)}, u32[]{:S(2)}, u32[]{:S(2)}) async-start(f32[32,1,1280]{2,1,0:T(1,128)} %bitcast.3), calls=%async_computation.1 | async-start | bytes 327680 | tf_op jit(solution)/shard_map/all_to_all | solution.py:392
  41.4 0.8 %shard_map.32.base = f32[1728,128]{1,0:T(8,128)S(1)} custom-call(f32[1728,128]{1,0:T(8,128)S(1)} %get-tuple-element.12.field, f32[1,128]{1,0:T(1,128)S(1)} %get-tuple-element.11.rate, f32[1728,128]{1,0:T(8,128)S(1)} %get-tuple-element.16.middle), custom_call_target="tpu_custom_call" | custom-call | flops 4000000 | bytes 2654720 | tf_op jit(solution)/shard_map/pallas_call | solution.py:357
  42.2 2.3 %all-to-all-done.1 = f32[32,1,1280]{2,1,0:T(1,128)S(1)} async-done(((f32[32,1,1280]{2,1,0:T(1,128)}), f32[32,1,1280]{2,1,0:T(1,128)S(1)}, u32[]{:S(2)}, u32[]{:S(2)}) %all-to-all-start.1) | async-done | bytes 163872 | tf_op jit(solution)/shard_map/all_to_all | solution.py:392
  44.5 0.0 collective-permute-done.1.halo
  44.5 1.2 %shard_map.33 = f32[1728,128]{1,0:T(8,128)} custom-call(f32[1,128]{1,0:T(1,128)S(1)} %get-tuple-element.11.rate, f32[584,128]{1,0:T(8,128)S(1)} %collective-permute-done.1.halo, f32[320,128]{1,0:T(8,128)S(1)} %bitcast.6, f32[1728,128]{1,0:T(8,128)S(1)} %shard_map.32.base), custom_call_target="tpu_custom_call" | custom-call | flops 4000000 | bytes 2232832 | tf_op jit(solution)/shard_map/pallas_call | solution.py:357
  (1 shorter events, 0.0 us)
Async XLA Ops:
  2.3 23.5 %collective-permute-start = (f32[576,128]{1,0:T(8,128)S(1)}, f32[576,128]{1,0:T(8,128)S(1)}, u32[]{:S(2)}, u32[]{:S(2)}) collective-permute-start(f32[576,128]{1,0:T(8,128)S(1)} %get-tuple-element.13), channel_id=1, source_target_pairs={{0,7},{1,0},{2,1},{3,2},{4,3},{5,4},{6,5},{7,6},{8,15},{9,8},{10,9... | collective-permute-start | bytes 884744 | tf_op jit(solution)/shard_map/ppermute | solution.py:411
  9.3 22.6 %all-to-all-start = ((f32[16,1,1536]{2,1,0:T(1,128)}), f32[16,1,1536]{2,1,0:T(1,128)S(1)}, u32[]{:S(2)}, u32[]{:S(2)}) async-start(f32[16,1,1536]{2,1,0:T(1,128)} %bitcast.1), calls=%async_computation | async-start | bytes 196608 | tf_op jit(solution)/shard_map/all_to_all | solution.py:392
  26.6 17.9 %collective-permute-start.1 = (f32[584,128]{1,0:T(8,128)S(1)}, f32[584,128]{1,0:T(8,128)S(1)}, u32[]{:S(2)}, u32[]{:S(2)}) collective-permute-start(f32[584,128]{1,0:T(8,128)S(1)} %get-tuple-element.14), channel_id=1, source_target_pairs={{0,7},{1,0},{2,1},{3,2},{4,3},{5,4},{6,5},{7,6},{8,15},{9,8},{10,9... | collective-permute-start | bytes 897032 | tf_op jit(solution)/shard_map/ppermute | solution.py:424
  32.6 11.9 %all-to-all-start.1 = ((f32[32,1,1280]{2,1,0:T(1,128)}), f32[32,1,1280]{2,1,0:T(1,128)S(1)}, u32[]{:S(2)}, u32[]{:S(2)}) async-start(f32[32,1,1280]{2,1,0:T(1,128)} %bitcast.3), calls=%async_computation.1 | async-start | bytes 327680 | tf_op jit(solution)/shard_map/all_to_all | solution.py:392

commit v5 on v3

--- a/solution.py
+++ b/solution.py
@@ -255,9 +255,10 @@
 
 def states(totals):
     density = totals[0]
-    flow = [t / density for t in totals[1:4]]
+    inverse = 1.0 / density
+    flow = [t * inverse for t in totals[1:4]]
     square = flow[0] * flow[0] + flow[1] * flow[1] + flow[2] * flow[2]
-    temper = (2.0 * totals[4] / density - square) / 3.0
+    temper = (2.0 * totals[4] * inverse - square) * (1.0 / 3.0)
     spread = 2.0 * math.pi * temper
     return flow, density / (spread * jnp.sqrt(spread)), 0.5 / temper
 

time: 46.1 us -> 46.1 us (level)
  no operation moved by 1% of the time
where the time goes in v5:
time: 46.1 us; the launch traced here: 45.8 us
  starting transfers between devices  35.5 us (77%)
  Pallas kernels  5.91 us (13%)
  waiting for transfers between devices  4.26 us (9%)
    all_to_all x2, starting transfers between devices, exchange(): lax.all_to_all(blocks.reshape(count, 1, -1), axis, 0, 0, axis_index_group...  25.3 us
    ppermute x2, starting transfers between devices, step(): halo = lax.ppermute(halo, ('vel', 'box'), downwind_pairs())  10.3 us
    pallas_call x6, Pallas kernels, call(): pl.pallas_call(kernel, out_shape=shapes, in_specs=[hbm if i in remote_in...  5.91 us
    all_to_all x2, waiting for transfers between devices, exchange(): lax.all_to_all(blocks.reshape(count, 1, -1), axis, 0, 0, axis_index_group...  4.26 us
  transfers between devices with their start and end apart: 4, of which 2 were waited for; matrix products, arithmetic and copies ran while one was open for 0% of the time, Pallas kernels for 5%

profile of v5, /device:TPU:1, one launch (start us, length us, event | category | flops | bytes accessed | tf_op | source)
XLA Modules:
  0.0 45.8 jit_solution(3355623974187896795)
XLA Ops:
  0.0 2.3 %shard_map.28 = (f32[576,128]{1,0:T(8,128)S(1)}, f32[192,128]{1,0:T(8,128)}, f32[1728,128]{1,0:T(8,128)S(1)}, f32[1,128]{1,0:T(1,128)S(1)}) custom-call(f32[1728,128]{1,0:T(8,128)} %bitcast.8, f32[1,128]{1,0:T(1,128)} %rate_hbm.1), custom_call_target="tpu_custom_call" | custom-call | flops 4000000 | bytes 2163712 | tf_op jit(solution)/shard_map/pallas_call | solution.py:357
  2.3 6.9 %collective-permute-start = (f32[576,128]{1,0:T(8,128)S(1)}, f32[576,128]{1,0:T(8,128)S(1)}, u32[]{:S(2)}, u32[]{:S(2)}) collective-permute-start(f32[576,128]{1,0:T(8,128)S(1)} %get-tuple-element.13), channel_id=1, source_target_pairs={{0,7},{1,0},{2,1},{3,2},{4,3},{5,4},{6,5},{7,6},{8,15},{9,8},{10,9... | collective-permute-start | bytes 884744 | tf_op jit(solution)/shard_map/ppermute | solution.py:411
  9.3 16.5 %all-to-all-start = ((f32[16,1,1536]{2,1,0:T(1,128)}), f32[16,1,1536]{2,1,0:T(1,128)S(1)}, u32[]{:S(2)}, u32[]{:S(2)}) async-start(f32[16,1,1536]{2,1,0:T(1,128)} %bitcast.1), calls=%async_computation | async-start | bytes 196608 | tf_op jit(solution)/shard_map/all_to_all | solution.py:392
  25.8 0.0 collective-permute-done.halo
  25.8 0.7 %shard_map.29 = (f32[1728,128]{1,0:T(8,128)S(1)}, f32[584,128]{1,0:T(8,128)S(1)}) custom-call(f32[1728,128]{1,0:T(8,128)S(1)} %get-tuple-element.12.field, f32[1,128]{1,0:T(1,128)S(1)} %get-tuple-element.11.rate, f32[576,128]{1,0:T(8,128)S(1)} %collective-permute-done.halo), custom_call_target="tpu_custom_call" | custom-call | flops 4000000 | bytes 2363904 | tf_op jit(solution)/shard_map/pallas_call | solution.py:357
  26.6 3.4 %collective-permute-start.1 = (f32[584,128]{1,0:T(8,128)S(1)}, f32[584,128]{1,0:T(8,128)S(1)}, u32[]{:S(2)}, u32[]{:S(2)}) collective-permute-start(f32[584,128]{1,0:T(8,128)S(1)} %get-tuple-element.14), channel_id=1, source_target_pairs={{0,7},{1,0},{2,1},{3,2},{4,3},{5,4},{6,5},{7,6},{8,15},{9,8},{10,9... | collective-permute-start | bytes 897032 | tf_op jit(solution)/shard_map/ppermute | solution.py:424
  29.9 1.9 %all-to-all-done = f32[16,1,1536]{2,1,0:T(1,128)S(1)} async-done(((f32[16,1,1536]{2,1,0:T(1,128)}), f32[16,1,1536]{2,1,0:T(1,128)S(1)}, u32[]{:S(2)}, u32[]{:S(2)}) %all-to-all-start) | async-done | bytes 98336 | tf_op jit(solution)/shard_map/all_to_all | solution.py:392
  31.9 0.7 %shard_map.31 = f32[320,128]{1,0:T(8,128)} custom-call(f32[192,128]{1,0:T(8,128)S(1)} %bitcast.7), custom_call_target="tpu_custom_call" | custom-call | flops 4000000 | bytes 262144 | tf_op jit(solution)/shard_map/pallas_call | solution.py:357
  32.6 8.8 %all-to-all-start.1 = ((f32[32,1,1280]{2,1,0:T(1,128)}), f32[32,1,1280]{2,1,0:T(1,128)S(1)}, u32[]{:S(2)}, u32[]{:S(2)}) async-start(f32[32,1,1280]{2,1,0:T(1,128)} %bitcast.3), calls=%async_computation.1 | async-start | bytes 327680 | tf_op jit(solution)/shard_map/all_to_all | solution.py:392
  41.4 0.8 %shard_map.32.base = f32[1728,128]{1,0:T(8,128)S(1)} custom-call(f32[1728,128]{1,0:T(8,128)S(1)} %get-tuple-element.12.field, f32[1,128]{1,0:T(1,128)S(1)} %get-tuple-element.11.rate, f32[1728,128]{1,0:T(8,128)S(1)} %get-tuple-element.16.middle), custom_call_target="tpu_custom_call" | custom-call | flops 4000000 | bytes 2654720 | tf_op jit(solution)/shard_map/pallas_call | solution.py:357
  42.2 2.3 %all-to-all-done.1 = f32[32,1,1280]{2,1,0:T(1,128)S(1)} async-done(((f32[32,1,1280]{2,1,0:T(1,128)}), f32[32,1,1280]{2,1,0:T(1,128)S(1)}, u32[]{:S(2)}, u32[]{:S(2)}) %all-to-all-start.1) | async-done | bytes 163872 | tf_op jit(solution)/shard_map/all_to_all | solution.py:392
  44.5 0.0 collective-permute-done.1.halo
  44.5 1.3 %shard_map.33 = f32[1728,128]{1,0:T(8,128)} custom-call(f32[1,128]{1,0:T(1,128)S(1)} %get-tuple-element.11.rate, f32[584,128]{1,0:T(8,128)S(1)} %collective-permute-done.1.halo, f32[320,128]{1,0:T(8,128)S(1)} %bitcast.6, f32[1728,128]{1,0:T(8,128)S(1)} %shard_map.32.base), custom_call_target="tpu_custom_call" | custom-call | flops 4000000 | bytes 2232832 | tf_op jit(solution)/shard_map/pallas_call | solution.py:357
  (1 shorter events, 0.0 us)
Async XLA Ops:
  2.3 23.5 %collective-permute-start = (f32[576,128]{1,0:T(8,128)S(1)}, f32[576,128]{1,0:T(8,128)S(1)}, u32[]{:S(2)}, u32[]{:S(2)}) collective-permute-start(f32[576,128]{1,0:T(8,128)S(1)} %get-tuple-element.13), channel_id=1, source_target_pairs={{0,7},{1,0},{2,1},{3,2},{4,3},{5,4},{6,5},{7,6},{8,15},{9,8},{10,9... | collective-permute-start | bytes 884744 | tf_op jit(solution)/shard_map/ppermute | solution.py:411
  9.3 22.6 %all-to-all-start = ((f32[16,1,1536]{2,1,0:T(1,128)}), f32[16,1,1536]{2,1,0:T(1,128)S(1)}, u32[]{:S(2)}, u32[]{:S(2)}) async-start(f32[16,1,1536]{2,1,0:T(1,128)} %bitcast.1), calls=%async_computation | async-start | bytes 196608 | tf_op jit(solution)/shard_map/all_to_all | solution.py:392
  26.6 17.9 %collective-permute-start.1 = (f32[584,128]{1,0:T(8,128)S(1)}, f32[584,128]{1,0:T(8,128)S(1)}, u32[]{:S(2)}, u32[]{:S(2)}) collective-permute-start(f32[584,128]{1,0:T(8,128)S(1)} %get-tuple-element.14), channel_id=1, source_target_pairs={{0,7},{1,0},{2,1},{3,2},{4,3},{5,4},{6,5},{7,6},{8,15},{9,8},{10,9... | collective-permute-start | bytes 897032 | tf_op jit(solution)/shard_map/ppermute | solution.py:424
  32.6 11.9 %all-to-all-start.1 = ((f32[32,1,1280]{2,1,0:T(1,128)}), f32[32,1,1280]{2,1,0:T(1,128)S(1)}, u32[]{:S(2)}, u32[]{:S(2)}) async-start(f32[32,1,1280]{2,1,0:T(1,128)} %bitcast.3), calls=%async_computation.1 | async-start | bytes 327680 | tf_op jit(solution)/shard_map/all_to_all | solution.py:392
